TPU v7x, 512 devices: a whole 4x4x16 slice. The times are simulated.
512 devices in a mesh: dp: 16 (over y, z_lo), seq: 32 (over z_hi, x, core).
Axes of the slice: x: 4, y: 4, z: 16 (z_hi: 4, z_lo: 4; z = z_hi * 4 + z_lo), core: 2. Of those that a mesh axis runs over, the one named last changes fastest.
Arguments:
- residual_stream: bfloat16 [65536, 512], P(('dp', 'seq')), parts along dimension 0, may hold values from -6 to 6
- norm_gain: float32 [512], replicated, may hold values from 0.5 to 1.5
- in_proj: bfloat16 [512, 2048], replicated, may hold values from -0.25 to 0.25
- conv_weight: float32 [4, 1024], replicated, may hold values from -3 to 3
- conv_bias: float32 [1024], replicated, may hold values from -0.5 to 0.5
- state_proj: bfloat16 [1024, 64], replicated, may hold values from -0.1875 to 0.1875
- step_proj: bfloat16 [32, 1024], replicated, may hold values from -1 to 1
- step_bias: float32 [1024], replicated, may hold values from -4 to 0
- decay_rate: float32 [1024, 16], replicated, may hold values from 0.0001 to 1
- skip_gain: float32 [1024], replicated, may hold values from 0.5 to 1.5
- out_proj: bfloat16 [1024, 512], replicated, may hold values from -0.1875 to 0.1875
Outputs:
- block_out: bfloat16 [65536, 512], P(('dp', 'seq')), parts along dimension 0
There are 16 independent parts, one for each index of `dp`. A program takes and returns all parts, laid end to end along the dimension named above; an argument that names none is the same for every part. Nothing has to cross between parts.
All inputs are finite; a program needn't handle non-finite values.
Results may differ from a plain program's by a relative error of at most 0.012.
Values may be sent and summed in bfloat16 or wider, within the bound.
A program may use at most 64 MiB of HBM per device.

v0:
```python
import math

import jax
import jax.numpy as jnp
from jax import lax
from jax.sharding import PartitionSpec as P


def prefix_2(part, axis, combine, identity):
    place = lax.axis_index(axis)
    gathered = jax.tree.map(lambda a: lax.all_gather(a, axis), part)
    state = jax.tree.map(lambda a, e: jnp.zeros_like(a) + jnp.asarray(e, a.dtype), part, identity)

    def one(lap, state):
        return combine(
            state, jax.tree.map(lambda a: lax.dynamic_index_in_dim(a, lap, 0, False), gathered)
        )

    return lax.fori_loop(0, place, one, state)


def swapped(value, axis, stride):
    mask = 2**stride
    pairs = [(source, source ^ mask) for source in range(lax.axis_size(axis))]
    return lax.ppermute(value, axis, pairs)


def passed_along(value, axis, steps):
    count = lax.axis_size(axis)
    initial, last = (max(0, -steps), min(count, count - steps))
    return lax.ppermute(value, axis, [(source, source + steps) for source in range(initial, last)])


def normalize(values, norm_gain):
    inv_scale = lax.rsqrt(jnp.mean(values * values, axis=-1, keepdims=True) + 1e-05)
    return (values * inv_scale * norm_gain).astype(jnp.bfloat16)


def prefix(totals, final_state, decay_rate):
    decay_whole = jnp.exp(-totals[..., None] * decay_rate)

    def combine(earlier, latter):
        return (earlier[0] * latter[0], earlier[1] * latter[0] + latter[1])

    identity = (jnp.ones_like(decay_whole), jnp.zeros_like(final_state))
    _, carry_in = prefix_2((decay_whole, final_state), "seq", combine, identity)
    return carry_in


def shards(
    residual_stream,
    norm_gain,
    in_proj,
    conv_weight,
    conv_bias,
    state_proj,
    step_proj,
    step_bias,
    decay_rate,
    skip_gain,
    out_proj,
):
    length = residual_stream.shape[0]
    inner_width = conv_weight.shape[1]
    kernel = conv_weight.shape[0]
    low_rank = step_proj.shape[0]
    states = decay_rate.shape[1]
    bit_count = lax.axis_size("seq").bit_length() - 1
    hidden = residual_stream.astype(jnp.float32)
    forward_norm = normalize(hidden, norm_gain)
    flipped_norm = normalize(hidden[::-1, ::-1], norm_gain)
    for bit_index in range(bit_count):
        flipped_norm = swapped(flipped_norm, "seq", bit_index)
    stacked = jnp.stack([forward_norm, flipped_norm], axis=1)
    joined = jnp.einsum("tbd,df->tbf", stacked, in_proj, preferred_element_type=jnp.float32).astype(
        jnp.bfloat16
    )
    inner_part = joined[:, :, :inner_width]
    gate_part = joined[:, :, inner_width:].astype(jnp.float32)
    last_rows = inner_part[length - kernel + 1 :]
    before = passed_along(last_rows, "seq", 1)
    padded = jnp.concatenate([before, inner_part], axis=0).astype(jnp.float32)
    conv_sum = conv_bias + jnp.zeros((length, 2, inner_width), jnp.float32)
    for offset in range(kernel):
        conv_sum = conv_sum + conv_weight[offset] * padded[offset : offset + length]
    activated = jax.nn.silu(conv_sum).astype(jnp.bfloat16)
    projected = jnp.einsum("tbe,ef->tbf", activated, state_proj, preferred_element_type=jnp.float32)
    step_low = projected[:, :, :low_rank].astype(jnp.bfloat16)
    input_map = projected[:, :, low_rank : low_rank + states]
    output_map = projected[:, :, low_rank + states :]
    step_size = jax.nn.softplus(
        jnp.einsum("tbr,re->tbe", step_low, step_proj, preferred_element_type=jnp.float32)
        + step_bias
    )
    signal = activated.astype(jnp.float32)

    def advance(carried, inputs):
        step_row, signal_row, input_row, output_row = inputs
        carried = (
            jnp.exp(-step_row[..., None] * decay_rate) * carried
            + (step_row * signal_row)[..., None] * input_row[:, None, :]
        )
        return (carried, jnp.sum(carried * output_row[:, None, :], axis=-1))

    final_state, scanned = lax.scan(
        advance,
        jnp.zeros((2, inner_width, states), jnp.float32),
        (step_size, signal, input_map, output_map),
        unroll=8,
    )
    positions = lax.broadcasted_iota(jnp.int32, (length, length), 0)
    sources = lax.broadcasted_iota(jnp.int32, (length, length), 1)
    lower_ones = (positions >= sources).astype(jnp.float32)
    cumulative = jnp.einsum("ts,sbe->tbe", lower_ones, step_size, precision=lax.Precision.HIGHEST)
    totals = cumulative[length - 1]
    carry_in = prefix(totals, final_state, decay_rate)
    block_rows = math.gcd(length, 64)

    def correct(pieces):
        cum_piece, map_piece = pieces
        return jnp.sum(
            jnp.exp(-cum_piece[..., None] * decay_rate) * map_piece[:, :, None, :] * carry_in[None],
            axis=-1,
        )

    correction = lax.map(
        correct,
        (
            cumulative.reshape(length // block_rows, block_rows, 2, inner_width),
            output_map.reshape(length // block_rows, block_rows, 2, states),
        ),
    )
    correction = correction.reshape(length, 2, inner_width)
    gated_mix = (scanned + correction + skip_gain * signal) * jax.nn.silu(gate_part)
    projected_out = jnp.einsum(
        "tbe,ed->tbd", gated_mix.astype(jnp.bfloat16), out_proj, preferred_element_type=jnp.float32
    ).astype(jnp.bfloat16)
    forward_out = projected_out[:, 0]
    flipped_out = projected_out[:, 1][::-1, ::-1]
    for bit_index in range(bit_count):
        flipped_out = swapped(flipped_out, "seq", bit_index)
    return (hidden + forward_out.astype(jnp.float32) + flipped_out.astype(jnp.float32)).astype(
        jnp.bfloat16
    )


def solution(mesh):
    return jax.shard_map(
        shards,
        mesh=mesh,
        in_specs=(P(("dp", "seq"), None), P(), P(), P(), P(), P(), P(), P(), P(), P(), P()),
        out_specs=P(("dp", "seq"), None),
        check_vma=False,
    )
```

profile of v0, /device:TPU:1, one launch (start us, length us, event | category | flops | bytes accessed | tf_op | source)
XLA Modules:
  0.0 435.5 jit_solution(8508982807113877300)
XLA Ops:
  6.5 1.9 rev.6
  8.5 1.0 multiply_reduce_fusion.10
  9.6 1.0 fusion.29
  10.7 8.7 %collective-permute-start = (bf16[128,512]{1,0:T(8,128)(2,1)S(1)}, bf16[128,512]{1,0:T(8,128)(2,1)S(1)}, u32[]{:S(2)}, u32[]{:S(2)}) collective-permute-start(bf16[128,512]{1,0:T(8,128)(2,1)S(1)} %get-tuple-element.332), channel_id=1, source_target_pairs={{0,1},{1,0},{2,3},{3,2},{4,5},{5,4},{6,7},{7,6},{8,9},{9,8},{10,11... | collective-permute-start | bytes 393224 | tf_op jit(solution)/shard_map/ppermute | solution.py:25
  19.4 1.0 collective-permute-done
  20.4 1.9 collective-permute-start.1
  22.3 4.7 %collective-permute-done.1 = bf16[128,512]{1,0:T(8,128)(2,1)S(1)} collective-permute-done((bf16[128,512]{1,0:T(8,128)(2,1)S(1)}, bf16[128,512]{1,0:T(8,128)(2,1)S(1)}, u32[]{:S(2)}, u32[]{:S(2)}) %collective-permute-start.1) | collective-permute-done | bytes 131104 | tf_op jit(solution)/shard_map/ppermute | solution.py:25
  27.0 1.9 collective-permute-start.2
  28.9 5.3 %collective-permute-done.2 = bf16[128,512]{1,0:T(8,128)(2,1)S(1)} collective-permute-done((bf16[128,512]{1,0:T(8,128)(2,1)S(1)}, bf16[128,512]{1,0:T(8,128)(2,1)S(1)}, u32[]{:S(2)}, u32[]{:S(2)}) %collective-permute-start.2) | collective-permute-done | bytes 131104 | tf_op jit(solution)/shard_map/ppermute | solution.py:25
  34.2 3.5 collective-permute-start.3
  37.6 13.7 %collective-permute-done.3 = bf16[128,512]{1,0:T(8,128)(2,1)S(1)} collective-permute-done((bf16[128,512]{1,0:T(8,128)(2,1)S(1)}, bf16[128,512]{1,0:T(8,128)(2,1)S(1)}, u32[]{:S(2)}, u32[]{:S(2)}) %collective-permute-start.3) | collective-permute-done | bytes 131104 | tf_op jit(solution)/shard_map/ppermute | solution.py:25
  51.4 12.1 %collective-permute-start.4 = (bf16[128,512]{1,0:T(8,128)(2,1)S(1)}, bf16[128,512]{1,0:T(8,128)(2,1)S(1)}, u32[]{:S(2)}, u32[]{:S(2)}) collective-permute-start(bf16[128,512]{1,0:T(8,128)(2,1)S(1)} %collective-permute-done.3), channel_id=1, source_target_pairs={{0,16},{1,17},{2,18},{3,19},{4,20},{5,21},{6,22},{7,23},{8,24},{9,... | collective-permute-start | bytes 393224 | tf_op jit(solution)/shard_map/ppermute | solution.py:25
  63.5 2.3 collective-permute-done.4
  65.8 0.7 convolution_convert_fusion
  66.5 1.1 copy-done.3
  67.6 14.4 %collective-permute-start.5 = (bf16[3,2,1024]{2,0,1:T(4,128)(2,1)S(1)}, bf16[3,2,1024]{2,0,1:T(4,128)(2,1)S(1)}, u32[]{:S(2)}, u32[]{:S(2)}) collective-permute-start(bf16[3,2,1024]{2,0,1:T(4,128)(2,1)S(1)} %slice.230), channel_id=1, source_target_pairs={{0,1},{1,2},{2,3},{3,4},{4,5},{5,6},{6,7},{7,8},{8,9},{9,10},{10,1... | collective-permute-start | bytes 36872 | tf_op jit(solution)/shard_map/ppermute | solution.py:31
  82.0 1.1 slice.231
  83.4 1.7 convert_bitcast_fusion
  85.9 1.0 copy-done.4
  86.9 1.6 fusion.22
  88.5 55.0 %while.37 = (s32[]{:T(128)}, f32[2,1024,16]{1,2,0:T(8,128)S(1)}, f32[16,8,2,1024]{3,1,0,2:T(8,128)}, f32[16,8,2,1024]{3,1,0,2:T(8,128)}, f32[1024,16]{0,1:T(8,12...) while((s32[]{:T(128)}, f32[2,1024,16]{1,2,0:T(8,128)S(1)}, ...), condition=%wide.region_11.12_spmd.clone, body=%wide.region_2.11_spmd.clone.sunk | while | flops 2441226 | bytes 1941052 | solution.py:105
  88.5 1.6 constant_dynamic-slice_fusion.38
  91.9 1.6 constant_dynamic-slice_fusion.38
  95.3 1.6 constant_dynamic-slice_fusion.38
  98.6 1.6 constant_dynamic-slice_fusion.38
  102.0 1.8 constant_dynamic-slice_fusion.38
  105.6 1.6 constant_dynamic-slice_fusion.38
  108.9 1.9 constant_dynamic-slice_fusion.38
  112.6 1.6 constant_dynamic-slice_fusion.38
  115.9 1.9 constant_dynamic-slice_fusion.38
  119.5 1.6 constant_dynamic-slice_fusion.38
  122.9 1.9 constant_dynamic-slice_fusion.38
  126.5 1.6 constant_dynamic-slice_fusion.38
  129.9 1.6 constant_dynamic-slice_fusion.38
  133.2 1.6 constant_dynamic-slice_fusion.38
  136.6 1.6 constant_dynamic-slice_fusion.38
  139.9 1.8 constant_dynamic-slice_fusion.38
  144.2 3.5 fusion.21
  147.7 0.8 slice_negate_fusion
  148.5 0.7 multiply_exponential_fusion
  149.4 91.0 %all-gather.6.cloned.1.call-done = f32[64,1024,16]{1,2,0:T(8,128)} async-done(((f32[2,1024,16]{1,2,0:T(8,128)}), f32[64,1024,16]{1,2,0:T(8,128)}) %all-gather.6.cloned.1.call-update) | async-done | bytes 4194320 | tf_op jit(solution)/shard_map/all_gather | solution.py:11
  240.4 92.1 %all-gather.4.cloned.1.call-done = f32[32,2,1024,16]{2,3,1,0:T(8,128)} async-done(((f32[1,2,1024,16]{2,3,1,0:T(8,128)}), f32[32,2,1024,16]{2,3,1,0:T(8,128)}) %all-gather.4.cloned.1.call-update) | async-done | bytes 4194320 | tf_op jit(solution)/shard_map/all_gather | solution.py:11
  332.5 1.1 while.35
  332.5 1.0 bitcast_add_fusion.3
  333.6 11.9 %while.36 = (s32[]{:T(128)}, f32[2,64,2,1024]{3,1,0,2:T(8,128)}, f32[2,64,2,1024]{3,1,0,2:T(8,128)}, f32[1024,16]{0,1:T(8,128)S(1)}, f32[2,64,2,16]{1,0,3,2:T(2,128)S(1)}, /*index=5*/f32[2,1024,16]{1,2,0:T(8,128)S(1)}, s32[]{:T(128)}) while((s32[]{:T(128)}, f32[2,64,2,1024]{3,1,0,2:T(8,128)}, f32[2,64,2,1024]{3,1,0,2:T(8,128)}, ...), condition=%wide.region_16.17_spmd, body=%wide.region_14.16_spmd.sunk | while | flops 8388610 | bytes 4432469 | solution.py:126
  333.6 1.1 dynamic-slice_negate_fusion.2
  335.2 3.3 multiply_reduce_fusion.15
  338.6 1.0 copy_dynamic-update-slice_fusion.4
  339.5 1.1 dynamic-slice_negate_fusion.2
  341.1 3.3 multiply_reduce_fusion.15
  344.5 1.0 copy_dynamic-update-slice_fusion.4
  345.5 2.1 fusion.12
  347.6 1.7 convolution_convert_fusion.1
  349.8 1.9 collective-permute-start.6
  351.7 1.3 collective-permute-done.6
  353.0 4.7 %collective-permute-start.7 = (bf16[128,512]{1,0:T(8,128)(2,1)S(1)}, bf16[128,512]{1,0:T(8,128)(2,1)S(1)}, u32[]{:S(2)}, u32[]{:S(2)}) collective-permute-start(bf16[128,512]{1,0:T(8,128)(2,1)S(1)} %collective-permute-done.6), channel_id=1, source_target_pairs={{0,2},{1,3},{2,0},{3,1},{4,6},{5,7},{6,4},{7,5},{8,10},{9,11},{10,... | collective-permute-start | bytes 393224 | tf_op jit(solution)/shard_map/ppermute | solution.py:25
  357.7 3.7 collective-permute-done.7
  361.4 8.6 %collective-permute-start.8 = (bf16[128,512]{1,0:T(8,128)(2,1)S(1)}, bf16[128,512]{1,0:T(8,128)(2,1)S(1)}, u32[]{:S(2)}, u32[]{:S(2)}) collective-permute-start(bf16[128,512]{1,0:T(8,128)(2,1)S(1)} %collective-permute-done.7), channel_id=1, source_target_pairs={{0,4},{1,5},{2,6},{3,7},{4,0},{5,1},{6,2},{7,3},{8,12},{9,13},{10,... | collective-permute-start | bytes 393224 | tf_op jit(solution)/shard_map/ppermute | solution.py:25
  370.0 3.1 collective-permute-done.8
  373.1 12.7 %collective-permute-start.9 = (bf16[128,512]{1,0:T(8,128)(2,1)S(1)}, bf16[128,512]{1,0:T(8,128)(2,1)S(1)}, u32[]{:S(2)}, u32[]{:S(2)}) collective-permute-start(bf16[128,512]{1,0:T(8,128)(2,1)S(1)} %collective-permute-done.8), channel_id=1, source_target_pairs={{0,8},{1,9},{2,10},{3,11},{4,12},{5,13},{6,14},{7,15},{8,0},{9,1},... | collective-permute-start | bytes 393224 | tf_op jit(solution)/shard_map/ppermute | solution.py:25
  385.8 8.5 %collective-permute-done.9 = bf16[128,512]{1,0:T(8,128)(2,1)S(1)} collective-permute-done((bf16[128,512]{1,0:T(8,128)(2,1)S(1)}, bf16[128,512]{1,0:T(8,128)(2,1)S(1)}, u32[]{:S(2)}, u32[]{:S(2)}) %collective-permute-start.9) | collective-permute-done | bytes 131104 | tf_op jit(solution)/shard_map/ppermute | solution.py:25
  394.3 23.1 %collective-permute-start.10 = (bf16[128,512]{1,0:T(8,128)(2,1)S(1)}, bf16[128,512]{1,0:T(8,128)(2,1)S(1)}, u32[]{:S(2)}, u32[]{:S(2)}) collective-permute-start(bf16[128,512]{1,0:T(8,128)(2,1)S(1)} %collective-permute-done.9), channel_id=1, source_target_pairs={{0,16},{1,17},{2,18},{3,19},{4,20},{5,21},{6,22},{7,23},{8,24},{9,... | collective-permute-start | bytes 393224 | tf_op jit(solution)/shard_map/ppermute | solution.py:25
  417.4 10.5 %collective-permute-done.10 = bf16[128,512]{1,0:T(8,128)(2,1)S(1)} collective-permute-done((bf16[128,512]{1,0:T(8,128)(2,1)S(1)}, bf16[128,512]{1,0:T(8,128)(2,1)S(1)}, u32[]{:S(2)}, u32[]{:S(2)}) %collective-permute-start.10) | collective-permute-done | bytes 131104 | tf_op jit(solution)/shard_map/ppermute | solution.py:25
  427.9 0.7 fusion.28
  (387 shorter events, 29.5 us)
Async XLA Ops:
  6.5 59.3 %copy-start = (bf16[512,2048]{1,0:T(8,128)(2,1)S(1)}, bf16[512,2048]{1,0:T(8,128)(2,1)}, u32[]{:S(2)}) copy-start(bf16[512,2048]{1,0:T(8,128)(2,1)} %param.19) | copy-start | bytes 6291460
  6.5 75.4 %copy-start.8 = (f32[4,1024]{1,0:T(4,128)S(1)}, f32[4,1024]{1,0:T(4,128)}, u32[]{:S(2)}) copy-start(f32[4,1024]{1,0:T(4,128)} %param.20) | copy-start | bytes 49156
  6.5 76.8 %copy-start.9 = (f32[1024]{0:T(1024)S(1)}, f32[1024]{0:T(1024)}, u32[]{:S(2)}) copy-start(f32[1024]{0:T(1024)} %param.21) | copy-start | bytes 12292
  6.5 233.9 %all-gather.6.cloned.1.call-start = ((), (), s32[]{:S(2)}) async-start(), calls=%async_computation.1 | async-start | bytes 4325376 | tf_op jit(solution)/shard_map/all_gather | solution.py:11
  10.7 9.7 %collective-permute-start = (bf16[128,512]{1,0:T(8,128)(2,1)S(1)}, bf16[128,512]{1,0:T(8,128)(2,1)S(1)}, u32[]{:S(2)}, u32[]{:S(2)}) collective-permute-start(bf16[128,512]{1,0:T(8,128)(2,1)S(1)} %get-tuple-element.332), channel_id=1, source_target_pairs={{0,1},{1,0},{2,3},{3,2},{4,5},{5,4},{6,7},{7,6},{8,9},{9,8},{10,11... | collective-permute-start | bytes 393224 | tf_op jit(solution)/shard_map/ppermute | solution.py:25
  20.4 6.6 %collective-permute-start.1 = (bf16[128,512]{1,0:T(8,128)(2,1)S(1)}, bf16[128,512]{1,0:T(8,128)(2,1)S(1)}, u32[]{:S(2)}, u32[]{:S(2)}) collective-permute-start(bf16[128,512]{1,0:T(8,128)(2,1)S(1)} %collective-permute-done), channel_id=1, source_target_pairs={{0,2},{1,3},{2,0},{3,1},{4,6},{5,7},{6,4},{7,5},{8,10},{9,11},{10,... | collective-permute-start | bytes 393224 | tf_op jit(solution)/shard_map/ppermute | solution.py:25
  27.0 7.2 %collective-permute-start.2 = (bf16[128,512]{1,0:T(8,128)(2,1)S(1)}, bf16[128,512]{1,0:T(8,128)(2,1)S(1)}, u32[]{:S(2)}, u32[]{:S(2)}) collective-permute-start(bf16[128,512]{1,0:T(8,128)(2,1)S(1)} %collective-permute-done.1), channel_id=1, source_target_pairs={{0,4},{1,5},{2,6},{3,7},{4,0},{5,1},{6,2},{7,3},{8,12},{9,13},{10,... | collective-permute-start | bytes 393224 | tf_op jit(solution)/shard_map/ppermute | solution.py:25
  34.2 17.2 %collective-permute-start.3 = (bf16[128,512]{1,0:T(8,128)(2,1)S(1)}, bf16[128,512]{1,0:T(8,128)(2,1)S(1)}, u32[]{:S(2)}, u32[]{:S(2)}) collective-permute-start(bf16[128,512]{1,0:T(8,128)(2,1)S(1)} %collective-permute-done.2), channel_id=1, source_target_pairs={{0,8},{1,9},{2,10},{3,11},{4,12},{5,13},{6,14},{7,15},{8,0},{9,1},... | collective-permute-start | bytes 393224 | tf_op jit(solution)/shard_map/ppermute | solution.py:25
  51.4 14.4 %collective-permute-start.4 = (bf16[128,512]{1,0:T(8,128)(2,1)S(1)}, bf16[128,512]{1,0:T(8,128)(2,1)S(1)}, u32[]{:S(2)}, u32[]{:S(2)}) collective-permute-start(bf16[128,512]{1,0:T(8,128)(2,1)S(1)} %collective-permute-done.3), channel_id=1, source_target_pairs={{0,16},{1,17},{2,18},{3,19},{4,20},{5,21},{6,22},{7,23},{8,24},{9,... | collective-permute-start | bytes 393224 | tf_op jit(solution)/shard_map/ppermute | solution.py:25
  66.5 1.1 copy-start.3
  67.6 15.6 %collective-permute-start.5 = (bf16[3,2,1024]{2,0,1:T(4,128)(2,1)S(1)}, bf16[3,2,1024]{2,0,1:T(4,128)(2,1)S(1)}, u32[]{:S(2)}, u32[]{:S(2)}) collective-permute-start(bf16[3,2,1024]{2,0,1:T(4,128)(2,1)S(1)} %slice.230), channel_id=1, source_target_pairs={{0,1},{1,2},{2,3},{3,4},{4,5},{5,6},{6,7},{7,8},{8,9},{9,10},{10,1... | collective-permute-start | bytes 36872 | tf_op jit(solution)/shard_map/ppermute | solution.py:31
  82.0 3.0 copy-start.6
  83.1 2.4 copy-start.7
  83.2 2.4 copy-start.10
  83.3 5.2 %copy-start.1 = (f32[1024,16]{0,1:T(8,128)S(1)}, f32[1024,16]{0,1:T(8,128)}, u32[]{:S(2)}) copy-start(f32[1024,16]{0,1:T(8,128)} %param.25) | copy-start | bytes 196612
  85.9 1.0 copy-start.4
  143.5 0.6 copy-start.2
  144.1 188.3 %all-gather.4.cloned.1.call-start = ((), (), s32[]{:S(2)}) async-start(), calls=%async_computation | async-start | bytes 4325376 | tf_op jit(solution)/shard_map/all_gather | solution.py:11
  333.6 11.9 %copy-start.11 = (f32[1024]{0:T(1024)S(1)}, f32[1024]{0:T(1024)}, u32[]{:S(2)}) copy-start(f32[1024]{0:T(1024)} %param.26) | copy-start | bytes 12292
  345.4 82.5 %copy-start.5 = (bf16[128,512]{1,0:T(8,128)(2,1)S(1)}, bf16[128,512]{1,0:T(8,128)(2,1)}, u32[]{:S(2)}) copy-start(bf16[128,512]{1,0:T(8,128)(2,1)} %param.17) | copy-start | bytes 393220
  349.8 3.2 collective-permute-start.6
  353.0 8.4 %collective-permute-start.7 = (bf16[128,512]{1,0:T(8,128)(2,1)S(1)}, bf16[128,512]{1,0:T(8,128)(2,1)S(1)}, u32[]{:S(2)}, u32[]{:S(2)}) collective-permute-start(bf16[128,512]{1,0:T(8,128)(2,1)S(1)} %collective-permute-done.6), channel_id=1, source_target_pairs={{0,2},{1,3},{2,0},{3,1},{4,6},{5,7},{6,4},{7,5},{8,10},{9,11},{10,... | collective-permute-start | bytes 393224 | tf_op jit(solution)/shard_map/ppermute | solution.py:25
  361.4 11.7 %collective-permute-start.8 = (bf16[128,512]{1,0:T(8,128)(2,1)S(1)}, bf16[128,512]{1,0:T(8,128)(2,1)S(1)}, u32[]{:S(2)}, u32[]{:S(2)}) collective-permute-start(bf16[128,512]{1,0:T(8,128)(2,1)S(1)} %collective-permute-done.7), channel_id=1, source_target_pairs={{0,4},{1,5},{2,6},{3,7},{4,0},{5,1},{6,2},{7,3},{8,12},{9,13},{10,... | collective-permute-start | bytes 393224 | tf_op jit(solution)/shard_map/ppermute | solution.py:25
  373.1 21.2 %collective-permute-start.9 = (bf16[128,512]{1,0:T(8,128)(2,1)S(1)}, bf16[128,512]{1,0:T(8,128)(2,1)S(1)}, u32[]{:S(2)}, u32[]{:S(2)}) collective-permute-start(bf16[128,512]{1,0:T(8,128)(2,1)S(1)} %collective-permute-done.8), channel_id=1, source_target_pairs={{0,8},{1,9},{2,10},{3,11},{4,12},{5,13},{6,14},{7,15},{8,0},{9,1},... | collective-permute-start | bytes 393224 | tf_op jit(solution)/shard_map/ppermute | solution.py:25
  394.3 33.7 %collective-permute-start.10 = (bf16[128,512]{1,0:T(8,128)(2,1)S(1)}, bf16[128,512]{1,0:T(8,128)(2,1)S(1)}, u32[]{:S(2)}, u32[]{:S(2)}) collective-permute-start(bf16[128,512]{1,0:T(8,128)(2,1)S(1)} %collective-permute-done.9), channel_id=1, source_target_pairs={{0,16},{1,17},{2,18},{3,19},{4,20},{5,21},{6,22},{7,23},{8,24},{9,... | collective-permute-start | bytes 393224 | tf_op jit(solution)/shard_map/ppermute | solution.py:25
Sparse Core Ops, SparseCore 0:
  144.3 96.0 all-gather.5
  243.5 88.8 all-gather.3
where the time goes:
time: 438 us; the launch traced here: 435 us
  waiting for transfers between devices  237 us (54%)
  starting transfers between devices  93.5 us (21%)
  local copies, waits for them, and re-layouts  48.7 us (11%)
  other arithmetic  33.8 us (8%)
  between operations  13.7 us (3%)
  matrix products  6.52 us (1%)
    all_gather x2, waiting for transfers between devices, prefix_2(): gathered = jax.tree.map(lambda a: lax.all_gather(a, axis), part)  183 us
    ppermute x10, starting transfers between devices, swapped(): return lax.ppermute(value, axis, pairs)  79.1 us
    ppermute x10, waiting for transfers between devices, swapped(): return lax.ppermute(value, axis, pairs)  54.1 us
    slice x32, local copies, waits for them, and re-layouts, shards(): lax.scan(advance, jnp.zeros((2, inner_width, states), jnp.float32), (step...  27.8 us
    ppermute x1, starting transfers between devices, passed_along(): lax.ppermute(value, axis, [(source, source + steps) for source in range(i...  14.4 us
    reduce_sum x48, other arithmetic, advance(): return (carried, jnp.sum(carried * output_row[:, None, :], axis=-1))  12.5 us
    dynamic_update_slice x16, local copies, waits for them, and re-layouts, shards(): lax.scan(advance, jnp.zeros((2, inner_width, states), jnp.float32), (step...  10.3 us
  transfers between devices with their start and end apart: 13, of which 12 were waited for; matrix products, arithmetic and copies ran while one was open for 1% of the time, Pallas kernels for 0%

commit v1 on v0

v1 whole, which is shorter than its diff:
```python
import functools
import math

import jax
import jax.numpy as jnp
from jax import lax
from jax.experimental import pallas as pl
from jax.experimental.pallas import tpu as pltpu
from jax.sharding import PartitionSpec as P

F32 = jnp.float32
BF16 = jnp.bfloat16
LOG2E = math.log2(math.e)
GROUP = 8
FAR = 4
LANES = 128
ROWS = 8


def dot(a, b):
    return jnp.dot(a, b, preferred_element_type=F32)


def split2(v):
    high = v.astype(BF16)
    return high, (v - high.astype(F32)).astype(BF16)


def anti_identity():
    row = lax.broadcasted_iota(jnp.int32, (LANES, LANES), 0)
    col = lax.broadcasted_iota(jnp.int32, (LANES, LANES), 1)
    return (row + col == LANES - 1).astype(F32).astype(BF16)


def flip_lanes(v, anti):
    pieces = [v[:, i : i + LANES] for i in range(0, v.shape[1], LANES)]
    return jnp.concatenate([dot(p, anti) for p in pieces[::-1]], axis=1)


def inv_rms(v):
    return lax.rsqrt(jnp.mean(v * v, axis=-1, keepdims=True) + 1e-05)


def softplus(v):
    return jnp.maximum(v, 0.0) + jnp.log1p(jnp.exp(-jnp.abs(v)))


def silu(v):
    return v * jax.nn.sigmoid(v)


def kernel(
    x_ref, gain_ref, in_ref, cw_ref, cb_ref, sp_ref, tp_ref, tb_ref, decay_ref, skip_ref, out_ref,
    o_ref,
    halo, nrm, a2, edge, u_s, proj, proj_t, dt_s, du_s, hist, cblk, cum, gc, pre, sg, gmix,
    send_a, recv_a, send_z, recv_z, send_c, recv_c, hin,
    halo_send, halo_recv, a_send, a_recv, z_send, z_recv, c_send, c_recv,
):
    tokens, width = x_ref.shape
    inner_width = cw_ref.shape[1]
    taps = cw_ref.shape[0]
    rank = tp_ref.shape[0]
    states = decay_ref.shape[1]
    blocks = tokens // ROWS
    slices = inner_width // LANES
    index = lax.axis_index("seq")
    count = GROUP * FAR
    far = index // GROUP
    place = index % GROUP
    left = (index + count - 1) % count
    right = (index + 1) % count
    members = [far * GROUP + (place + d) % GROUP for d in range(1, GROUP)]
    distant = [((far + d) % FAR) * GROUP + place for d in range(1, FAR)]

    barrier = pltpu.get_barrier_semaphore()
    for peer in [left, right] + members + distant:
        pl.semaphore_signal(
            barrier, inc=1, device_id={"seq": peer}, device_id_type=pl.DeviceIdType.MESH
        )

    def remote(src, dst, send, recv, peer):
        return pltpu.make_async_remote_copy(
            src_ref=src, dst_ref=dst, send_sem=send, recv_sem=recv,
            device_id={"seq": peer}, device_id_type=pl.DeviceIdType.MESH,
        )

    row = lax.broadcasted_iota(jnp.int32, (states, states), 0)
    col = lax.broadcasted_iota(jnp.int32, (states, states), 1)
    unit = (row == col).astype(F32).astype(BF16)
    rates = decay_ref[...]
    p1 = rates.astype(BF16)
    rest = rates - p1.astype(F32)
    p2 = rest.astype(BF16)
    p3 = (rest - p2.astype(F32)).astype(BF16)
    across = (((1,), (1,)), ((), ()))
    turned = sum(
        lax.dot_general(unit, p, across, preferred_element_type=F32) for p in (p1, p2, p3)
    )
    turned = turned * (-LOG2E)
    for k in range(slices):
        a2[k] = turned[:, k * LANES : (k + 1) * LANES]

    def a2_wide(first=0, last=slices):
        return jnp.concatenate([a2[k] for k in range(first, last)], axis=1)

    anti = anti_identity()
    gain = gain_ref[...]
    x = x_ref[...]
    x32 = x.astype(F32)
    scale = inv_rms(x32)
    nrm[0] = (x32 * scale * gain).astype(BF16)
    nrm[1] = (flip_lanes(x, anti) * scale * gain).astype(BF16)

    def convolve(v, branch, cols):
        total = cb_ref[:, cols]
        size = v.shape[0]
        for k in range(taps):
            back = taps - 1 - k
            shift = back if branch == 0 else (size - back) % size
            moved = v if back == 0 else pltpu.roll(v, shift, 0)
            total = total + cw_ref[k : k + 1, cols] * moved
        return silu(total).astype(BF16)

    wide = 256

    def front(i, _):
        cols = pl.ds(pl.multiple_of(i * wide, wide), wide)
        for branch in range(2):
            inner = dot(nrm[branch], in_ref[:, cols])
            edge[branch, :, cols] = inner[:ROWS] if branch == 0 else inner[tokens - ROWS :]
            u_s[branch, :, cols] = convolve(inner, branch, cols).astype(F32)
        return 0

    lax.fori_loop(0, inner_width // wide, front, 0)

    for branch in range(2):
        proj[branch] = dot(u_s[branch].astype(BF16), sp_ref[...])

    def steps(i, _):
        cols = pl.ds(pl.multiple_of(i * wide, wide), wide)
        for branch in range(2):
            low = proj[branch, :, :rank].astype(BF16)
            dt = softplus(dot(low, tp_ref[:, cols]) + tb_ref[:, cols])
            dt_s[branch, :, cols] = dt
            du_s[branch, :, cols] = dt * u_s[branch, :, cols]
        return 0

    lax.fori_loop(0, inner_width // wide, steps, 0)

    pl.semaphore_wait(barrier, 2 + len(members) + len(distant))
    edge_rows = halo.shape[1]
    to_right = remote(
        x_ref.at[pl.ds(tokens - edge_rows, edge_rows)], halo.at[0], halo_send.at[0], halo_recv.at[0], right
    )
    to_left = remote(x_ref.at[pl.ds(0, edge_rows)], halo.at[1], halo_send.at[1], halo_recv.at[1], left)
    to_right.start()
    to_left.start()

    def turn_proj():
        proj_t[...] = jnp.concatenate([proj[0], proj[1]], axis=1).T

    proj_width = proj.shape[2]
    turn_proj()
    half = slices // 2

    def scan(first, last):
        ends = []
        for part in range(2):
            lanes = pl.ds(part * half * LANES, half * LANES)
            rate = a2_wide(part * half, (part + 1) * half)

            def chunk(c, carried, lanes=lanes, rate=rate):
                carried = list(carried)
                base = c * ROWS
                rolled = [
                    pltpu.roll(proj_t[rank : rank + states, :], (tokens - base) % tokens, 1),
                    pltpu.roll(
                        proj_t[proj_width + rank : proj_width + rank + states, :],
                        (base + ROWS) % tokens, 1,
                    ),
                ]
                for j in range(ROWS):
                    for branch in range(2):
                        t = base + j if branch == 0 else tokens - 1 - base - j
                        pick = j if branch == 0 else ROWS - 1 - j
                        column = jnp.broadcast_to(rolled[branch][:, pick : pick + 1], (states, LANES))
                        column = jnp.concatenate([column] * half, axis=1)
                        dt = jnp.broadcast_to(dt_s[branch, pl.ds(t, 1), lanes], (states, half * LANES))
                        du = jnp.broadcast_to(du_s[branch, pl.ds(t, 1), lanes], (states, half * LANES))
                        h = jnp.exp2(dt * rate) * carried[branch] + du * column
                        hist[branch, pl.ds(pl.multiple_of(t * states, states), states), lanes] = h.astype(BF16)
                        carried[branch] = h
                return tuple(carried)

            zero = jnp.zeros((states, half * LANES), F32)
            ends.append(lax.fori_loop(first, last, chunk, (zero, zero)))
        return ends

    main = scan(1, blocks)
    for part in range(2):
        for branch in range(2):
            for k in range(half):
                hin[branch, part * half + k] = main[part][branch][:, k * LANES : (k + 1) * LANES]

    to_right.wait()
    to_left.wait()
    border = halo[...]
    near = border[0].astype(F32)
    far_side = border[1]
    far32 = far_side.astype(F32)
    ahead = (near * inv_rms(near) * gain).astype(BF16)
    behind = (flip_lanes(far_side, anti) * inv_rms(far32) * gain).astype(BF16)
    has_left = (index > 0).astype(F32)
    has_right = (index < count - 1).astype(F32)

    def border_front(i, _):
        cols = pl.ds(pl.multiple_of(i * wide, wide), wide)
        weights = in_ref[:, cols]
        v = dot(ahead, weights)[edge_rows - ROWS :] * has_left
        joined = jnp.concatenate([v, edge[0, :, cols]], axis=0)
        u_s[0, 0:ROWS, cols] = convolve(joined, 0, cols).astype(F32)[ROWS:]
        v = dot(behind, weights)[:ROWS] * has_right
        joined = jnp.concatenate([edge[1, :, cols], v], axis=0)
        u_s[1, tokens - ROWS : tokens, cols] = convolve(joined, 1, cols).astype(F32)[:ROWS]
        return 0

    lax.fori_loop(0, inner_width // wide, border_front, 0)
    border_u = jnp.concatenate([u_s[0, 0:ROWS], u_s[1, tokens - ROWS : tokens]], axis=0)
    border_p = dot(border_u.astype(BF16), sp_ref[...])
    proj[0, 0:ROWS] = border_p[:ROWS]
    proj[1, tokens - ROWS : tokens] = border_p[ROWS:]
    border_dt = softplus(dot(border_p[:, :rank].astype(BF16), tp_ref[...]) + tb_ref[...])
    border_du = border_dt * border_u
    dt_s[0, 0:ROWS] = border_dt[:ROWS]
    dt_s[1, tokens - ROWS : tokens] = border_dt[ROWS:]
    du_s[0, 0:ROWS] = border_du[:ROWS]
    du_s[1, tokens - ROWS : tokens] = border_du[ROWS:]
    turn_proj()
    start = scan(0, 1)

    def wide_tile(rows):
        return jnp.concatenate(rows + [jnp.zeros((16 - len(rows), LANES), F32)], axis=0)

    main_tot = [
        jnp.sum(dt_s[0, ROWS:tokens], axis=0, keepdims=True),
        jnp.sum(dt_s[1, 0 : tokens - ROWS], axis=0, keepdims=True),
    ]
    start_tot = [
        jnp.sum(border_dt[:ROWS], axis=0, keepdims=True),
        jnp.sum(border_dt[ROWS:], axis=0, keepdims=True),
    ]

    def tot_rows(values):
        rows = []
        for v in values:
            high = v.astype(BF16).astype(F32)
            rows += [high, v - high]
        return wide_tile(rows).astype(BF16)

    for k in range(slices):
        lanes = slice(k * LANES, (k + 1) * LANES)
        part, inside = divmod(k, half)
        own = slice(inside * LANES, (inside + 1) * LANES)
        for branch in range(2):
            first = start[part][branch][:, own]
            grown = jnp.exp2(main_tot[branch][:, lanes] * a2[k]) * first + hin[branch, k]
            send_a[k, branch] = grown.astype(BF16)
            hist_keep = first
            hin[branch, k] = hist_keep
        send_a[k, 2] = tot_rows([(main_tot[b] + start_tot[b])[:, lanes] for b in range(2)])

    copies_a = []
    for d, peer in enumerate(members):
        target = (place + d + 1) % GROUP
        copies_a.append(
            remote(send_a.at[target], recv_a.at[place], a_send.at[d], a_recv.at[d], peer)
        )
    for c in copies_a:
        c.start()
    recv_a[place] = send_a[place]
    recv_z[far] = jnp.zeros(recv_z.shape[1:], BF16)

    def gates(i, _):
        cols = pl.ds(pl.multiple_of(i * wide, wide), wide)
        behind_cols = pl.ds(pl.multiple_of(inner_width + i * wide, wide), wide)
        for branch in range(2):
            sg[branch, :, cols] = silu(dot(nrm[branch], in_ref[:, behind_cols]))
        return 0

    lax.fori_loop(0, inner_width // wide, gates, 0)

    for c in copies_a:
        c.wait()

    rate = a2[place]
    got_s = [[recv_a[m, b].astype(F32) for m in range(GROUP)] for b in range(2)]
    got_t = []
    for m in range(GROUP):
        rows = recv_a[m, 2].astype(F32)
        got_t.append([rows[0:1] + rows[1:2], rows[2:3] + rows[3:4]])

    prefix = [[None] * GROUP, [None] * GROUP]
    before = [[None] * GROUP, [None] * GROUP]
    for branch in range(2):
        state = jnp.zeros((states, LANES), F32)
        total = jnp.zeros((1, LANES), F32)
        order = range(GROUP) if branch == 0 else range(GROUP - 1, -1, -1)
        for m in order:
            prefix[branch][m] = state
            before[branch][m] = total
            state = jnp.exp2(got_t[m][branch] * rate) * state + got_s[branch][m]
            total = total + got_t[m][branch]
        send_z[branch, 0] = state.astype(BF16)
        send_z[branch, 1] = tot_rows([total])

    copies_z = []
    for d, peer in enumerate(distant):
        target = (far + d + 1) % FAR
        branch = (target < far).astype(jnp.int32)
        copies_z.append(
            remote(send_z.at[branch], recv_z.at[far], z_send.at[d], z_recv.at[d], peer)
        )
    for c in copies_z:
        c.start()

    t_row = lax.broadcasted_iota(jnp.int32, (tokens, tokens), 0)
    t_col = lax.broadcasted_iota(jnp.int32, (tokens, tokens), 1)
    below = [
        (t_col <= t_row) & ((t_col < ROWS) == (t_row < ROWS)),
        (t_col >= t_row) & ((t_col >= tokens - ROWS) == (t_row >= tokens - ROWS)),
    ]
    for branch in range(2):
        ones = below[branch].astype(F32).astype(BF16)
        high, low = split2(dt_s[branch])
        cum[branch] = dot(ones, high) + dot(ones, low)

    c_first = rank + states
    pick_row = lax.broadcasted_iota(jnp.int32, (states, 256), 0)
    pick_col = lax.broadcasted_iota(jnp.int32, (states, 256), 1)
    spread = (pick_col % states == pick_row).astype(F32).astype(BF16)
    own_row = lax.broadcasted_iota(jnp.int32, (tokens, 256), 0)
    own_col = lax.broadcasted_iota(jnp.int32, (tokens, 256), 1)
    own = own_col // states == own_row % (256 // states)
    for branch in range(2):
        maps = proj[branch, :, c_first : c_first + states].astype(BF16)
        cblk[branch] = jnp.where(own, dot(maps, spread), 0.0).astype(BF16)

    run = 256 // states

    def local_out(i, _):
        rows = pl.ds(pl.multiple_of(i * run, run), run)
        deep = pl.ds(pl.multiple_of(i * 256, 256), 256)
        for branch in range(2):
            local = dot(cblk[branch, rows, :], hist[branch, deep, :])
            pre[branch, rows, :] = local + skip_ref[...] * u_s[branch, rows, :]
        return 0

    lax.fori_loop(0, tokens // run, local_out, 0)

    def factors(i, _):
        rows = pl.ds(pl.multiple_of(i * ROWS, ROWS), ROWS)
        for branch in range(2):
            maps = proj[branch, rows, :]
            for n in range(states):
                c_col = jnp.broadcast_to(maps[:, c_first + n : c_first + n + 1], (ROWS, LANES))
                for k in range(slices):
                    seen = cum[branch, rows, k * LANES : (k + 1) * LANES]
                    gc[branch, k, n, rows, :] = jnp.exp2(seen * a2[k, n : n + 1, :]) * c_col
        return 0

    lax.fori_loop(0, blocks, factors, 0)

    for c in copies_z:
        c.wait()

    for branch in range(2):
        state = jnp.zeros((states, LANES), F32)
        order = range(FAR) if branch == 0 else range(FAR - 1, -1, -1)
        for z in order:
            here = (z < far) if branch == 0 else (z > far)
            rows = recv_z[z, 1].astype(F32)
            later = jnp.exp2((rows[0:1] + rows[1:2]) * rate) * state + recv_z[z, 0].astype(F32)
            state = jnp.where(here, later, state)
        for m in range(GROUP):
            entering = jnp.exp2(before[branch][m] * rate) * state + prefix[branch][m]
            send_c[m, branch] = entering.astype(BF16)

    copies_c = []
    for d, peer in enumerate(members):
        target = (place + d + 1) % GROUP
        copies_c.append(
            remote(send_c.at[target], recv_c.at[place], c_send.at[d], c_recv.at[d], peer)
        )
    for c in copies_c:
        c.start()
    recv_c[place] = send_c[place]
    for c in copies_c:
        c.wait()

    for branch in range(2):
        for k in range(slices):
            entering = recv_c[k, branch].astype(F32)
            gone = jnp.exp2(start_tot[branch][:, k * LANES : (k + 1) * LANES] * a2[k])
            hin[branch, k] = gone * entering + hin[branch, k]

    def finish(k, _):
        cols = pl.ds(pl.multiple_of(k * LANES, LANES), LANES)
        for branch in range(2):
            spread_h = [
                jnp.broadcast_to(hin[branch, k, n : n + 1, :], (ROWS, LANES)) for n in range(states)
            ]
            edge_h = recv_c[k, branch].astype(F32)
            border_block = 0 if branch == 0 else blocks - 1
            pieces = []
            for b in range(blocks):
                rows = slice(b * ROWS, (b + 1) * ROWS)
                total = pre[branch, rows, cols]
                for n in range(states):
                    if b == border_block:
                        h = jnp.broadcast_to(edge_h[n : n + 1, :], (ROWS, LANES))
                    else:
                        h = spread_h[n]
                    total = total + gc[branch, k, n, rows, :] * h
                pieces.append(total * sg[branch, rows, cols])
                if len(pieces) == 2:
                    gmix[branch, (b - 1) * ROWS : (b + 1) * ROWS, cols] = jnp.concatenate(
                        pieces, axis=0
                    ).astype(BF16)
                    pieces = []
        return 0

    lax.fori_loop(0, slices, finish, 0)
    forward = dot(gmix[0], out_ref[...]).astype(BF16)
    flipped = flip_lanes(dot(gmix[1], out_ref[...]).astype(BF16), anti)
    o_ref[...] = (x_ref[...].astype(F32) + forward.astype(F32) + flipped).astype(BF16)


def shards(
    residual_stream, norm_gain, in_proj, conv_weight, conv_bias, state_proj, step_proj,
    step_bias, decay_rate, skip_gain, out_proj,
):
    tokens, width = residual_stream.shape
    inner_width = conv_weight.shape[1]
    states = decay_rate.shape[1]
    slices = inner_width // LANES
    vmem = pl.BlockSpec(memory_space=pltpu.VMEM)
    by_token = (2, tokens, inner_width)
    scratch = [
        pltpu.VMEM((2, 16, width), BF16),
        pltpu.VMEM((2, tokens, width), BF16),
        pltpu.VMEM((slices, states, LANES), F32),
        pltpu.VMEM((2, ROWS, inner_width), F32),
        pltpu.VMEM(by_token, F32),
        pltpu.VMEM((2, tokens, state_proj.shape[1]), F32),
        pltpu.VMEM((2 * state_proj.shape[1], tokens), F32),
        pltpu.VMEM(by_token, F32),
        pltpu.VMEM(by_token, F32),
        pltpu.VMEM((2, tokens * states, inner_width), BF16),
        pltpu.VMEM((2, tokens, 256), BF16),
        pltpu.VMEM(by_token, F32),
        pltpu.VMEM((2, slices, states, tokens, LANES), F32),
        pltpu.VMEM(by_token, F32),
        pltpu.VMEM(by_token, F32),
        pltpu.VMEM(by_token, BF16),
        pltpu.VMEM((GROUP, 3, states, LANES), BF16),
        pltpu.VMEM((GROUP, 3, states, LANES), BF16),
        pltpu.VMEM((2, 2, states, LANES), BF16),
        pltpu.VMEM((FAR, 2, states, LANES), BF16),
        pltpu.VMEM((GROUP, 2, states, LANES), BF16),
        pltpu.VMEM((GROUP, 2, states, LANES), BF16),
        pltpu.VMEM((2, slices, states, LANES), F32),
        pltpu.SemaphoreType.DMA((2,)),
        pltpu.SemaphoreType.DMA((2,)),
        pltpu.SemaphoreType.DMA((GROUP - 1,)),
        pltpu.SemaphoreType.DMA((GROUP - 1,)),
        pltpu.SemaphoreType.DMA((FAR - 1,)),
        pltpu.SemaphoreType.DMA((FAR - 1,)),
        pltpu.SemaphoreType.DMA((GROUP - 1,)),
        pltpu.SemaphoreType.DMA((GROUP - 1,)),
    ]
    return pl.pallas_call(
        kernel,
        out_shape=jax.ShapeDtypeStruct((tokens, width), BF16),
        in_specs=[vmem] * 11,
        out_specs=vmem,
        scratch_shapes=scratch,
        compiler_params=pltpu.CompilerParams(
            collective_id=0, has_side_effects=True, vmem_limit_bytes=60 << 20
        ),
    )(
        residual_stream,
        norm_gain.reshape(1, -1),
        in_proj,
        conv_weight,
        conv_bias.reshape(1, -1),
        state_proj,
        step_proj,
        step_bias.reshape(1, -1),
        decay_rate,
        skip_gain.reshape(1, -1),
        out_proj,
    )


def solution(mesh):
    return jax.shard_map(
        shards,
        mesh=mesh,
        in_specs=(P(("dp", "seq"), None), P(), P(), P(), P(), P(), P(), P(), P(), P(), P()),
        out_specs=P(("dp", "seq"), None),
        check_vma=False,
    )
```

time: 438 us -> 48.3 us (0.11)
  waiting for transfers between devices: 237 us -> 0 us
  starting transfers between devices: 93.5 us -> 0 us
  local copies, waits for them, and re-layouts: 48.7 us -> 5.14 us
  Pallas kernels: 0 us -> 42.9 us
  other arithmetic: 33.8 us -> 0 us
  between operations: 13.7 us -> 0.01 us
  matrix products: 6.52 us -> 0 us
    all_gather x2 -> x0, waiting for transfers between devices: 183 us -> none  [prefix_2(): gathered = jax.tree.map(lambda a: lax.all_gather(a, axis), part)]
    ppermute x11 -> x0, starting transfers between devices: 93.4 us -> none  [the longest x10 79.1 us: swapped(): return lax.ppermute(value, axis, pairs)]
    ppermute x11 -> x0, waiting for transfers between devices: 54.2 us -> none  [the longest x10 54.1 us: swapped(): return lax.ppermute(value, axis, pairs)]
    pallas_call x0 -> x1, Pallas kernels: none -> 42.9 us  [shards(): pl.pallas_call(kernel, out_shape=jax.ShapeDtypeStruct((tokens, width), BF...]
    slice x38 -> x0, local copies, waits for them, and re-layouts: 29.2 us -> none  [the longest x32 27.8 us: shards(): lax.scan(advance, jnp.zeros((2, inner_width, states), jnp.float32), (step...]
    reduce_sum x52 -> x0, other arithmetic: 20.3 us -> none  [the longest x48 12.5 us: advance(): return (carried, jnp.sum(carried * output_row[:, None, :], axis=-1))]
    dynamic_update_slice x18 -> x0, local copies, waits for them, and re-layouts: 12.3 us -> none  [the longest x16 10.3 us: shards(): lax.scan(advance, jnp.zeros((2, inner_width, states), jnp.float32), (step...]
    dot_general x5 -> x0, matrix products: 6.52 us -> none  [the longest x1 3.48 us: shards(): jnp.einsum('ts,sbe->tbe', lower_ones, step_size, precision=lax.Precision....]
  transfers between devices with their start and end apart: 13 -> 0, of which waited for: 12 -> 0; matrix products, arithmetic and copies ran while one was open for 1% -> 0% of each run, Pallas kernels for 0% -> 0%
where the time goes in v1:
time: 48.3 us; the launch traced here: 48.1 us
  Pallas kernels  42.9 us (89%)
  local copies, waits for them, and re-layouts  5.14 us (11%)
    pallas_call x1, Pallas kernels, shards(): pl.pallas_call(kernel, out_shape=jax.ShapeDtypeStruct((tokens, width), BF...  42.9 us
    unnamed x3, local copies, waits for them, and re-layouts  5.14 us

profile of v1, /device:TPU:1, one launch (start us, length us, event | category | flops | bytes accessed | tf_op | source)
XLA Modules:
  0.0 48.1 jit_solution(17713784617099359267)
XLA Ops:
  0.0 1.7 %copy.12.sp_ref = bf16[1024,64]{1,0:T(8,128)(2,1)} copy(bf16[1024,64]{0,1:T(8,128)(2,1)} %param.16) | data formatting | bytes 262144 | tf_op args[5]
  1.7 1.8 %copy.13.decay_ref = f32[1024,16]{1,0:T(8,128)} copy(f32[1024,16]{0,1:T(8,128)} %param.19) | data formatting | bytes 131072 | tf_op args[8]
  3.6 42.9 %shard_map.109 = bf16[128,512]{1,0:T(8,128)(2,1)} custom-call(bf16[128,512]{1,0:T(8,128)(2,1)} %x_ref.1, f32[1,512]{1,0:T(1,128)} %bitcast.7, bf16[512,2048]{1,0:T(8,128)(2,1)} %in_ref.1, f32[4,1024]{1,0:T(4,128)} %cw_ref.1, f32[1,1024]{1,0:T(1,128)} %bitcast.4, bf16[1024,64]{1,0:T(8,128)(2,1)} %copy.12.sp_ref, bf16[32,1024]{1,0:T(8,128)(2,1)} %tp_ref.1, ...), custom_call_target="tpu_custom_call" | custom-call | tf_op jit(solution)/shard_map/pallas_call | solution.py:481
  46.5 1.6 %copy.15 = bf16[128,512]{1,0:T(8,128)(2,1)} copy(bf16[128,512]{1,0:T(8,128)(2,1)} %shard_map.109) | data formatting | bytes 262144

commit v2 on v1

--- a/solution.py
+++ b/solution.py
@@ -21,6 +21,10 @@
     return jnp.dot(a, b, preferred_element_type=F32)
 
 
+def dot_nt(a, b):
+    return lax.dot_general(a, b, (((1,), (1,)), ((), ())), preferred_element_type=F32)
+
+
 def split2(v):
     high = v.astype(BF16)
     return high, (v - high.astype(F32)).astype(BF16)
@@ -50,17 +54,18 @@
 
 
 def kernel(
-    x_ref, gain_ref, in_ref, cw_ref, cb_ref, sp_ref, tp_ref, tb_ref, decay_ref, skip_ref, out_ref,
+    x_hbm, gain_hbm, in_hbm, cw_hbm, cb_hbm, sp_hbm, tp_hbm, tb_hbm, decay_hbm, skip_hbm, out_hbm,
     o_ref,
+    x_ref, gain_ref, in_ref, gate_ref, cw_ref, cb_ref, sp_ref, tp_ref, tb_ref, decay_ref, skip_ref, out_ref,
     halo, nrm, a2, edge, u_s, proj, proj_t, dt_s, du_s, hist, cblk, cum, gc, pre, sg, gmix,
     send_a, recv_a, send_z, recv_z, send_c, recv_c, hin,
-    halo_send, halo_recv, a_send, a_recv, z_send, z_recv, c_send, c_recv,
+    halo_send, halo_recv, a_send, a_recv, z_send, z_recv, c_send, c_recv, fetched, go,
 ):
     tokens, width = x_ref.shape
     inner_width = cw_ref.shape[1]
     taps = cw_ref.shape[0]
     rank = tp_ref.shape[0]
-    states = decay_ref.shape[1]
+    states = decay_ref.shape[0]
     blocks = tokens // ROWS
     slices = inner_width // LANES
     index = lax.axis_index("seq")
@@ -73,7 +78,8 @@
     distant = [((far + d) % FAR) * GROUP + place for d in range(1, FAR)]
 
     barrier = pltpu.get_barrier_semaphore()
-    for peer in [left, right] + members + distant:
+    near_z = [distant[0], distant[2]]
+    for peer in [left, right] + members + near_z:
         pl.semaphore_signal(
             barrier, inc=1, device_id={"seq": peer}, device_id_type=pl.DeviceIdType.MESH
         )
@@ -84,21 +90,21 @@
             device_id={"seq": peer}, device_id_type=pl.DeviceIdType.MESH,
         )
 
-    row = lax.broadcasted_iota(jnp.int32, (states, states), 0)
-    col = lax.broadcasted_iota(jnp.int32, (states, states), 1)
-    unit = (row == col).astype(F32).astype(BF16)
-    rates = decay_ref[...]
-    p1 = rates.astype(BF16)
-    rest = rates - p1.astype(F32)
-    p2 = rest.astype(BF16)
-    p3 = (rest - p2.astype(F32)).astype(BF16)
-    across = (((1,), (1,)), ((), ()))
-    turned = sum(
-        lax.dot_general(unit, p, across, preferred_element_type=F32) for p in (p1, p2, p3)
-    )
-    turned = turned * (-LOG2E)
-    for k in range(slices):
-        a2[k] = turned[:, k * LANES : (k + 1) * LANES]
+    halves = [in_hbm.at[:, pl.ds(i * inner_width, inner_width)] for i in range(2)]
+    pairs = [
+        (x_hbm, x_ref), (gain_hbm, gain_ref), (halves[0], in_ref), (cw_hbm, cw_ref), (cb_hbm, cb_ref),
+        (sp_hbm, sp_ref), (tp_hbm, tp_ref), (tb_hbm, tb_ref), (decay_hbm, decay_ref),
+        (halves[1], gate_ref), (skip_hbm, skip_ref), (out_hbm, out_ref),
+    ]
+    fetches = [pltpu.make_async_copy(src, dst, fetched.at[i]) for i, (src, dst) in enumerate(pairs)]
+    for f in fetches:
+        f.start()
+
+    def arrive(first, last):
+        for f in fetches[first:last]:
+            f.wait()
+
+    arrive(0, 2)
 
     def a2_wide(first=0, last=slices):
         return jnp.concatenate([a2[k] for k in range(first, last)], axis=1)
@@ -122,6 +128,9 @@
         return silu(total).astype(BF16)
 
     wide = 256
+    arrive(2, 9)
+    for k in range(slices):
+        a2[k] = decay_ref[:, k * LANES : (k + 1) * LANES] * (-LOG2E)
 
     def front(i, _):
         cols = pl.ds(pl.multiple_of(i * wide, wide), wide)
@@ -134,7 +143,7 @@
     lax.fori_loop(0, inner_width // wide, front, 0)
 
     for branch in range(2):
-        proj[branch] = dot(u_s[branch].astype(BF16), sp_ref[...])
+        proj[branch] = dot_nt(u_s[branch].astype(BF16), sp_ref[...])
 
     def steps(i, _):
         cols = pl.ds(pl.multiple_of(i * wide, wide), wide)
@@ -147,14 +156,16 @@
 
     lax.fori_loop(0, inner_width // wide, steps, 0)
 
-    pl.semaphore_wait(barrier, 2 + len(members) + len(distant))
+    pl.semaphore_wait(barrier, 2 + len(members) + len(near_z))
     edge_rows = halo.shape[1]
     to_right = remote(
-        x_ref.at[pl.ds(tokens - edge_rows, edge_rows)], halo.at[0], halo_send.at[0], halo_recv.at[0], right
+        x_hbm.at[pl.ds(tokens - edge_rows, edge_rows)], halo.at[0], halo_send.at[0], halo_recv.at[0], right
     )
-    to_left = remote(x_ref.at[pl.ds(0, edge_rows)], halo.at[1], halo_send.at[1], halo_recv.at[1], left)
+    to_left = remote(x_hbm.at[pl.ds(0, edge_rows)], halo.at[1], halo_send.at[1], halo_recv.at[1], left)
     to_right.start()
     to_left.start()
+    for peer in near_z:
+        pl.semaphore_signal(go, inc=1, device_id={"seq": peer}, device_id_type=pl.DeviceIdType.MESH)
 
     def turn_proj():
         proj_t[...] = jnp.concatenate([proj[0], proj[1]], axis=1).T
@@ -226,7 +237,7 @@
 
     lax.fori_loop(0, inner_width // wide, border_front, 0)
     border_u = jnp.concatenate([u_s[0, 0:ROWS], u_s[1, tokens - ROWS : tokens]], axis=0)
-    border_p = dot(border_u.astype(BF16), sp_ref[...])
+    border_p = dot_nt(border_u.astype(BF16), sp_ref[...])
     proj[0, 0:ROWS] = border_p[:ROWS]
     proj[1, tokens - ROWS : tokens] = border_p[ROWS:]
     border_dt = softplus(dot(border_p[:, :rank].astype(BF16), tp_ref[...]) + tb_ref[...])
@@ -280,11 +291,12 @@
     recv_a[place] = send_a[place]
     recv_z[far] = jnp.zeros(recv_z.shape[1:], BF16)
 
+    arrive(9, len(fetches))
+
     def gates(i, _):
         cols = pl.ds(pl.multiple_of(i * wide, wide), wide)
-        behind_cols = pl.ds(pl.multiple_of(inner_width + i * wide, wide), wide)
-        for branch in range(2):
-            sg[branch, :, cols] = silu(dot(nrm[branch], in_ref[:, behind_cols]))
+        for branch in range(2):
+            sg[branch, :, cols] = silu(dot(nrm[branch], gate_ref[:, cols]))
         return 0
 
     lax.fori_loop(0, inner_width // wide, gates, 0)
@@ -313,6 +325,7 @@
         send_z[branch, 0] = state.astype(BF16)
         send_z[branch, 1] = tot_rows([total])
 
+    pl.semaphore_wait(go, len(near_z))
     copies_z = []
     for d, peer in enumerate(distant):
         target = (far + d + 1) % FAR
@@ -432,7 +445,7 @@
     lax.fori_loop(0, slices, finish, 0)
     forward = dot(gmix[0], out_ref[...]).astype(BF16)
     flipped = flip_lanes(dot(gmix[1], out_ref[...]).astype(BF16), anti)
-    o_ref[...] = (x_ref[...].astype(F32) + forward.astype(F32) + flipped).astype(BF16)
+    o_ref[...] = forward.astype(F32) + flipped
 
 
 def shards(
@@ -442,10 +455,25 @@
     tokens, width = residual_stream.shape
     inner_width = conv_weight.shape[1]
     states = decay_rate.shape[1]
+    rank = step_proj.shape[0]
+    columns = state_proj.shape[1]
     slices = inner_width // LANES
+    hbm = pl.BlockSpec(memory_space=pl.ANY)
     vmem = pl.BlockSpec(memory_space=pltpu.VMEM)
     by_token = (2, tokens, inner_width)
     scratch = [
+        pltpu.VMEM((tokens, width), BF16),
+        pltpu.VMEM((1, width), F32),
+        pltpu.VMEM((width, inner_width), BF16),
+        pltpu.VMEM((width, inner_width), BF16),
+        pltpu.VMEM(conv_weight.shape, F32),
+        pltpu.VMEM((1, inner_width), F32),
+        pltpu.VMEM((columns, inner_width), BF16),
+        pltpu.VMEM((rank, inner_width), BF16),
+        pltpu.VMEM((1, inner_width), F32),
+        pltpu.VMEM((states, inner_width), F32),
+        pltpu.VMEM((1, inner_width), F32),
+        pltpu.VMEM((inner_width, width), BF16),
         pltpu.VMEM((2, 16, width), BF16),
         pltpu.VMEM((2, tokens, width), BF16),
         pltpu.VMEM((slices, states, LANES), F32),
@@ -477,11 +505,13 @@
         pltpu.SemaphoreType.DMA((FAR - 1,)),
         pltpu.SemaphoreType.DMA((GROUP - 1,)),
         pltpu.SemaphoreType.DMA((GROUP - 1,)),
+        pltpu.SemaphoreType.DMA((12,)),
+        pltpu.SemaphoreType.REGULAR,
     ]
-    return pl.pallas_call(
+    mixed = pl.pallas_call(
         kernel,
-        out_shape=jax.ShapeDtypeStruct((tokens, width), BF16),
-        in_specs=[vmem] * 11,
+        out_shape=jax.ShapeDtypeStruct((tokens, width), F32),
+        in_specs=[hbm] * 11,
         out_specs=vmem,
         scratch_shapes=scratch,
         compiler_params=pltpu.CompilerParams(
@@ -493,13 +523,14 @@
         in_proj,
         conv_weight,
         conv_bias.reshape(1, -1),
-        state_proj,
+        state_proj.T,
         step_proj,
         step_bias.reshape(1, -1),
-        decay_rate,
+        decay_rate.T,
         skip_gain.reshape(1, -1),
         out_proj,
     )
+    return (residual_stream.astype(F32) + mixed).astype(BF16)
 
 
 def solution(mesh):

time: 48.3 us -> 43.2 us (0.89)
  local copies, waits for them, and re-layouts: 5.14 us -> 0.01 us
  other arithmetic: 0 us -> 1.63 us
  Pallas kernels: 42.9 us -> 41.4 us
    unnamed x3 -> x2, local copies, waits for them, and re-layouts: 5.14 us -> 0.01 us
    convert_element_type x0 -> x1, other arithmetic: none -> 1.63 us  [shards(): return (residual_stream.astype(F32) + mixed).astype(BF16)]
    pallas_call x1, Pallas kernels: 42.9 us -> 41.4 us  [shards(): pl.pallas_call(kernel, out_shape=jax.ShapeDtypeStruct((tokens, width), F3...]
where the time goes in v2:
time: 43.2 us; the launch traced here: 43 us
  Pallas kernels  41.4 us (96%)
  other arithmetic  1.63 us (4%)
    pallas_call x1, Pallas kernels, shards(): pl.pallas_call(kernel, out_shape=jax.ShapeDtypeStruct((tokens, width), F3...  41.4 us
    convert_element_type x1, other arithmetic, shards(): return (residual_stream.astype(F32) + mixed).astype(BF16)  1.63 us

profile of v2, /device:TPU:1, one launch (start us, length us, event | category | flops | bytes accessed | tf_op | source)
XLA Modules:
  0.0 43.0 jit_solution(3137172399353639508)
XLA Ops:
  0.0 0.0 copy-start
  0.0 41.4 %shard_map.109 = f32[128,512]{1,0:T(8,128)} custom-call(bf16[128,512]{1,0:T(8,128)(2,1)} %x_hbm.1, f32[1,512]{1,0:T(1,128)} %bitcast.11, bf16[512,2048]{1,0:T(8,128)(2,1)} %in_hbm.1, f32[4,1024]{1,0:T(4,128)} %cw_hbm.1, f32[1,1024]{1,0:T(1,128)} %bitcast.8, bf16[64,1024]{1,0:T(8,128)(2,1)} %bitcast.6, bf16[32,1024]{1,0:T(8,128)(2,1)} %tp_hbm.1, ...), custom_call_target="tpu_custom_call" | custom-call | tf_op jit(solution)/shard_map/pallas_call | solution.py:511
  41.4 0.0 copy-done
  41.4 1.6 %add_convert_fusion = bf16[128,512]{1,0:T(8,128)(2,1)} fusion(f32[128,512]{1,0:T(8,128)} %shard_map.109, bf16[128,512]{1,0:T(8,128)(2,1)S(1)} %copy-done), kind=kLoop, calls=%fused_computation | loop fusion | flops 196608 | bytes 524288 | tf_op jit(solution)/shard_map/convert_element_type | solution.py:533
Async XLA Ops:
  0.0 41.4 %copy-start = (bf16[128,512]{1,0:T(8,128)(2,1)S(1)}, bf16[128,512]{1,0:T(8,128)(2,1)}, u32[]{:S(2)}) copy-start(bf16[128,512]{1,0:T(8,128)(2,1)} %x_hbm.1) | copy-start | bytes 393220

commit v3 on v2

--- a/solution.py
+++ b/solution.py
@@ -15,6 +15,8 @@
 FAR = 4
 LANES = 128
 ROWS = 8
+SCAN = 40
+EARLY = 7
 
 
 def dot(a, b):
@@ -58,7 +60,7 @@
     o_ref,
     x_ref, gain_ref, in_ref, gate_ref, cw_ref, cb_ref, sp_ref, tp_ref, tb_ref, decay_ref, skip_ref, out_ref,
     halo, nrm, a2, edge, u_s, proj, proj_t, dt_s, du_s, hist, cblk, cum, gc, pre, sg, gmix,
-    send_a, recv_a, send_z, recv_z, send_c, recv_c, hin,
+    send_a, recv_a, send_z, recv_z, send_c, recv_c, hin, first_tot,
     halo_send, halo_recv, a_send, a_recv, z_send, z_recv, c_send, c_recv, fetched, go,
 ):
     tokens, width = x_ref.shape
@@ -151,7 +153,7 @@
             low = proj[branch, :, :rank].astype(BF16)
             dt = softplus(dot(low, tp_ref[:, cols]) + tb_ref[:, cols])
             dt_s[branch, :, cols] = dt
-            du_s[branch, :, cols] = dt * u_s[branch, :, cols]
+            du_s[branch, :, cols] = (dt * u_s[branch, :, cols]).astype(BF16)
         return 0
 
     lax.fori_loop(0, inner_width // wide, steps, 0)
@@ -174,7 +176,9 @@
     turn_proj()
     half = slices // 2
 
-    def scan(first, last):
+    lane = lax.broadcasted_iota(jnp.int32, (states, tokens), 1)
+
+    def scan(first, last, size):
         ends = []
         for part in range(2):
             lanes = pl.ds(part * half * LANES, half * LANES)
@@ -182,32 +186,30 @@
 
             def chunk(c, carried, lanes=lanes, rate=rate):
                 carried = list(carried)
-                base = c * ROWS
-                rolled = [
-                    pltpu.roll(proj_t[rank : rank + states, :], (tokens - base) % tokens, 1),
-                    pltpu.roll(
-                        proj_t[proj_width + rank : proj_width + rank + states, :],
-                        (base + ROWS) % tokens, 1,
-                    ),
-                ]
-                for j in range(ROWS):
+                base = first * ROWS + c * size
+                times = [[base + j, tokens - 1 - base - j] for j in range(size)]
+                added = []
+                for branch in range(2):
+                    top = branch * proj_width + rank
+                    maps = proj_t[top : top + states, :]
+                    tiles = [jnp.where(lane == t[branch], maps, 0.0).astype(BF16) for t in times]
+                    added.append(dot(jnp.concatenate(tiles, axis=0), du_s[branch, :, lanes]))
+                for j in range(size):
                     for branch in range(2):
-                        t = base + j if branch == 0 else tokens - 1 - base - j
-                        pick = j if branch == 0 else ROWS - 1 - j
-                        column = jnp.broadcast_to(rolled[branch][:, pick : pick + 1], (states, LANES))
-                        column = jnp.concatenate([column] * half, axis=1)
+                        t = times[j][branch]
                         dt = jnp.broadcast_to(dt_s[branch, pl.ds(t, 1), lanes], (states, half * LANES))
-                        du = jnp.broadcast_to(du_s[branch, pl.ds(t, 1), lanes], (states, half * LANES))
-                        h = jnp.exp2(dt * rate) * carried[branch] + du * column
+                        new = added[branch][j * states : (j + 1) * states]
+                        h = jnp.exp2(dt * rate) * carried[branch] + new
                         hist[branch, pl.ds(pl.multiple_of(t * states, states), states), lanes] = h.astype(BF16)
                         carried[branch] = h
                 return tuple(carried)
 
             zero = jnp.zeros((states, half * LANES), F32)
-            ends.append(lax.fori_loop(first, last, chunk, (zero, zero)))
+            trips = (last - first) * ROWS // size
+            ends.append(lax.fori_loop(0, trips, chunk, (zero, zero)))
         return ends
 
-    main = scan(1, blocks)
+    main = scan(1, blocks, SCAN)
     for part in range(2):
         for branch in range(2):
             for k in range(half):
@@ -244,10 +246,11 @@
     border_du = border_dt * border_u
     dt_s[0, 0:ROWS] = border_dt[:ROWS]
     dt_s[1, tokens - ROWS : tokens] = border_dt[ROWS:]
-    du_s[0, 0:ROWS] = border_du[:ROWS]
-    du_s[1, tokens - ROWS : tokens] = border_du[ROWS:]
+    none = jnp.zeros((tokens - ROWS, inner_width), F32)
+    du_s[0] = jnp.concatenate([border_du[:ROWS], none], axis=0).astype(BF16)
+    du_s[1] = jnp.concatenate([none, border_du[ROWS:]], axis=0).astype(BF16)
     turn_proj()
-    start = scan(0, 1)
+    start = scan(0, 1, ROWS)
 
     def wide_tile(rows):
         return jnp.concatenate(rows + [jnp.zeros((16 - len(rows), LANES), F32)], axis=0)
@@ -279,6 +282,8 @@
             hist_keep = first
             hin[branch, k] = hist_keep
         send_a[k, 2] = tot_rows([(main_tot[b] + start_tot[b])[:, lanes] for b in range(2)])
+        for branch in range(2):
+            first_tot[k, branch] = jnp.broadcast_to(start_tot[branch][:, lanes], (ROWS, LANES))
 
     copies_a = []
     for d, peer in enumerate(members):
@@ -300,6 +305,53 @@
         return 0
 
     lax.fori_loop(0, inner_width // wide, gates, 0)
+
+    t_row = lax.broadcasted_iota(jnp.int32, (tokens, tokens), 0)
+    t_col = lax.broadcasted_iota(jnp.int32, (tokens, tokens), 1)
+    below = [
+        (t_col <= t_row) & ((t_col < ROWS) == (t_row < ROWS)),
+        (t_col >= t_row) & ((t_col >= tokens - ROWS) == (t_row >= tokens - ROWS)),
+    ]
+    for branch in range(2):
+        ones = below[branch].astype(F32).astype(BF16)
+        high, low = split2(dt_s[branch])
+        cum[branch] = dot(ones, high) + dot(ones, low)
+
+    c_first = rank + states
+    pick_row = lax.broadcasted_iota(jnp.int32, (states, 256), 0)
+    pick_col = lax.broadcasted_iota(jnp.int32, (states, 256), 1)
+    spread = (pick_col % states == pick_row).astype(F32).astype(BF16)
+    own_row = lax.broadcasted_iota(jnp.int32, (tokens, 256), 0)
+    own_col = lax.broadcasted_iota(jnp.int32, (tokens, 256), 1)
+    own = own_col // states == own_row % (256 // states)
+    for branch in range(2):
+        maps = proj[branch, :, c_first : c_first + states].astype(BF16)
+        cblk[branch] = jnp.where(own, dot(maps, spread), 0.0).astype(BF16)
+
+    run = 256 // states
+
+    def local_out(i, _):
+        rows = pl.ds(pl.multiple_of(i * run, run), run)
+        deep = pl.ds(pl.multiple_of(i * 256, 256), 256)
+        for branch in range(2):
+            local = dot(cblk[branch, rows, :], hist[branch, deep, :])
+            pre[branch, rows, :] = local + skip_ref[...] * u_s[branch, rows, :]
+        return 0
+
+    lax.fori_loop(0, tokens // run, local_out, 0)
+
+    def factors(i, _):
+        rows = pl.ds(pl.multiple_of(i * ROWS, ROWS), ROWS)
+        for branch in range(2):
+            maps = proj[branch, rows, :]
+            for n in range(states):
+                c_col = jnp.broadcast_to(maps[:, c_first + n : c_first + n + 1], (ROWS, LANES))
+                for k in range(slices):
+                    seen = cum[branch, rows, k * LANES : (k + 1) * LANES]
+                    gc[branch, k, n, rows, :] = jnp.exp2(seen * a2[k, n : n + 1, :]) * c_col
+        return 0
+
+    lax.fori_loop(0, EARLY, factors, 0)
 
     for c in copies_a:
         c.wait()
@@ -336,52 +388,7 @@
     for c in copies_z:
         c.start()
 
-    t_row = lax.broadcasted_iota(jnp.int32, (tokens, tokens), 0)
-    t_col = lax.broadcasted_iota(jnp.int32, (tokens, tokens), 1)
-    below = [
-        (t_col <= t_row) & ((t_col < ROWS) == (t_row < ROWS)),
-        (t_col >= t_row) & ((t_col >= tokens - ROWS) == (t_row >= tokens - ROWS)),
-    ]
-    for branch in range(2):
-        ones = below[branch].astype(F32).astype(BF16)
-        high, low = split2(dt_s[branch])
-        cum[branch] = dot(ones, high) + dot(ones, low)
-
-    c_first = rank + states
-    pick_row = lax.broadcasted_iota(jnp.int32, (states, 256), 0)
-    pick_col = lax.broadcasted_iota(jnp.int32, (states, 256), 1)
-    spread = (pick_col % states == pick_row).astype(F32).astype(BF16)
-    own_row = lax.broadcasted_iota(jnp.int32, (tokens, 256), 0)
-    own_col = lax.broadcasted_iota(jnp.int32, (tokens, 256), 1)
-    own = own_col // states == own_row % (256 // states)
-    for branch in range(2):
-        maps = proj[branch, :, c_first : c_first + states].astype(BF16)
-        cblk[branch] = jnp.where(own, dot(maps, spread), 0.0).astype(BF16)
-
-    run = 256 // states
-
-    def local_out(i, _):
-        rows = pl.ds(pl.multiple_of(i * run, run), run)
-        deep = pl.ds(pl.multiple_of(i * 256, 256), 256)
-        for branch in range(2):
-            local = dot(cblk[branch, rows, :], hist[branch, deep, :])
-            pre[branch, rows, :] = local + skip_ref[...] * u_s[branch, rows, :]
-        return 0
-
-    lax.fori_loop(0, tokens // run, local_out, 0)
-
-    def factors(i, _):
-        rows = pl.ds(pl.multiple_of(i * ROWS, ROWS), ROWS)
-        for branch in range(2):
-            maps = proj[branch, rows, :]
-            for n in range(states):
-                c_col = jnp.broadcast_to(maps[:, c_first + n : c_first + n + 1], (ROWS, LANES))
-                for k in range(slices):
-                    seen = cum[branch, rows, k * LANES : (k + 1) * LANES]
-                    gc[branch, k, n, rows, :] = jnp.exp2(seen * a2[k, n : n + 1, :]) * c_col
-        return 0
-
-    lax.fori_loop(0, blocks, factors, 0)
+    lax.fori_loop(EARLY, blocks, factors, 0)
 
     for c in copies_z:
         c.wait()
@@ -398,31 +405,23 @@
             entering = jnp.exp2(before[branch][m] * rate) * state + prefix[branch][m]
             send_c[m, branch] = entering.astype(BF16)
 
-    copies_c = []
-    for d, peer in enumerate(members):
-        target = (place + d + 1) % GROUP
-        copies_c.append(
-            remote(send_c.at[target], recv_c.at[place], c_send.at[d], c_recv.at[d], peer)
+    def back(d):
+        target = (place + d) % GROUP
+        return remote(
+            send_c.at[target], recv_c.at[place], c_send.at[d - 1], c_recv.at[d - 1], far * GROUP + target
         )
-    for c in copies_c:
-        c.start()
+
+    for d in range(1, GROUP):
+        back(d).start()
     recv_c[place] = send_c[place]
-    for c in copies_c:
-        c.wait()
-
-    for branch in range(2):
-        for k in range(slices):
-            entering = recv_c[k, branch].astype(F32)
-            gone = jnp.exp2(start_tot[branch][:, k * LANES : (k + 1) * LANES] * a2[k])
-            hin[branch, k] = gone * entering + hin[branch, k]
-
-    def finish(k, _):
+
+    def finish(k):
         cols = pl.ds(pl.multiple_of(k * LANES, LANES), LANES)
         for branch in range(2):
-            spread_h = [
-                jnp.broadcast_to(hin[branch, k, n : n + 1, :], (ROWS, LANES)) for n in range(states)
-            ]
             edge_h = recv_c[k, branch].astype(F32)
+            gone = jnp.exp2(first_tot[k, branch, 0:1, :] * a2[k])
+            main_h = gone * edge_h + hin[branch, k]
+            spread_h = [jnp.broadcast_to(main_h[n : n + 1, :], (ROWS, LANES)) for n in range(states)]
             border_block = 0 if branch == 0 else blocks - 1
             pieces = []
             for b in range(blocks):
@@ -440,9 +439,14 @@
                         pieces, axis=0
                     ).astype(BF16)
                     pieces = []
-        return 0
-
-    lax.fori_loop(0, slices, finish, 0)
+
+    def finish_next(d, _):
+        back(d).wait()
+        finish((place + GROUP - d) % GROUP)
+        return 0
+
+    finish(place)
+    lax.fori_loop(1, GROUP, finish_next, 0)
     forward = dot(gmix[0], out_ref[...]).astype(BF16)
     flipped = flip_lanes(dot(gmix[1], out_ref[...]).astype(BF16), anti)
     o_ref[...] = forward.astype(F32) + flipped
@@ -482,7 +486,7 @@
         pltpu.VMEM((2, tokens, state_proj.shape[1]), F32),
         pltpu.VMEM((2 * state_proj.shape[1], tokens), F32),
         pltpu.VMEM(by_token, F32),
-        pltpu.VMEM(by_token, F32),
+        pltpu.VMEM(by_token, BF16),
         pltpu.VMEM((2, tokens * states, inner_width), BF16),
         pltpu.VMEM((2, tokens, 256), BF16),
         pltpu.VMEM(by_token, F32),
@@ -497,6 +501,7 @@
         pltpu.VMEM((GROUP, 2, states, LANES), BF16),
         pltpu.VMEM((GROUP, 2, states, LANES), BF16),
         pltpu.VMEM((2, slices, states, LANES), F32),
+        pltpu.VMEM((slices, 2, ROWS, LANES), F32),
         pltpu.SemaphoreType.DMA((2,)),
         pltpu.SemaphoreType.DMA((2,)),
         pltpu.SemaphoreType.DMA((GROUP - 1,)),

time: 43.2 us -> 41.3 us (0.956)
  Pallas kernels: 41.4 us -> 39.5 us
    pallas_call x1, Pallas kernels: 41.4 us -> 39.5 us  [shards(): pl.pallas_call(kernel, out_shape=jax.ShapeDtypeStruct((tokens, width), F3...]
where the time goes in v3:
time: 41.3 us; the launch traced here: 41.1 us
  Pallas kernels  39.5 us (96%)
  other arithmetic  1.63 us (4%)
    pallas_call x1, Pallas kernels, shards(): pl.pallas_call(kernel, out_shape=jax.ShapeDtypeStruct((tokens, width), F3...  39.5 us
    convert_element_type x1, other arithmetic, shards(): return (residual_stream.astype(F32) + mixed).astype(BF16)  1.63 us

profile of v3, /device:TPU:1, one launch (start us, length us, event | category | flops | bytes accessed | tf_op | source)
XLA Modules:
  0.0 41.1 jit_solution(12352804036738737744)
XLA Ops:
  0.0 0.0 copy-start
  0.0 39.5 %shard_map.109 = f32[128,512]{1,0:T(8,128)} custom-call(bf16[128,512]{1,0:T(8,128)(2,1)} %x_hbm.1, f32[1,512]{1,0:T(1,128)} %bitcast.11, bf16[512,2048]{1,0:T(8,128)(2,1)} %in_hbm.1, f32[4,1024]{1,0:T(4,128)} %cw_hbm.1, f32[1,1024]{1,0:T(1,128)} %bitcast.8, bf16[64,1024]{1,0:T(8,128)(2,1)} %bitcast.6, bf16[32,1024]{1,0:T(8,128)(2,1)} %tp_hbm.1, ...), custom_call_target="tpu_custom_call" | custom-call | tf_op jit(solution)/shard_map/pallas_call | solution.py:516
  39.5 0.0 copy-done
  39.5 1.6 %add_convert_fusion = bf16[128,512]{1,0:T(8,128)(2,1)} fusion(f32[128,512]{1,0:T(8,128)} %shard_map.109, bf16[128,512]{1,0:T(8,128)(2,1)S(1)} %copy-done), kind=kLoop, calls=%fused_computation | loop fusion | flops 196608 | bytes 524288 | tf_op jit(solution)/shard_map/convert_element_type | solution.py:538
Async XLA Ops:
  0.0 39.5 %copy-start = (bf16[128,512]{1,0:T(8,128)(2,1)S(1)}, bf16[128,512]{1,0:T(8,128)(2,1)}, u32[]{:S(2)}) copy-start(bf16[128,512]{1,0:T(8,128)(2,1)} %x_hbm.1) | copy-start | bytes 393220

commit v4 on v3

--- a/solution.py
+++ b/solution.py
@@ -15,6 +15,7 @@
 FAR = 4
 LANES = 128
 ROWS = 8
+FARTHEST = (4, 3, 5, 2, 6, 1, 7)
 SCAN = 40
 EARLY = 7
 
@@ -60,7 +61,7 @@
     o_ref,
     x_ref, gain_ref, in_ref, gate_ref, cw_ref, cb_ref, sp_ref, tp_ref, tb_ref, decay_ref, skip_ref, out_ref,
     halo, nrm, a2, edge, u_s, proj, proj_t, dt_s, du_s, hist, cblk, cum, gc, pre, sg, gmix,
-    send_a, recv_a, send_z, recv_z, send_c, recv_c, hin, first_tot,
+    send_a, recv_a, send_z, recv_z, send_c, recv_c, hin, first_tot, main_gone,
     halo_send, halo_recv, a_send, a_recv, z_send, z_recv, c_send, c_recv, fetched, go,
 ):
     tokens, width = x_ref.shape
@@ -99,7 +100,7 @@
         (halves[1], gate_ref), (skip_hbm, skip_ref), (out_hbm, out_ref),
     ]
     fetches = [pltpu.make_async_copy(src, dst, fetched.at[i]) for i, (src, dst) in enumerate(pairs)]
-    for f in fetches:
+    for f in fetches[:9]:
         f.start()
 
     def arrive(first, last):
@@ -131,6 +132,8 @@
 
     wide = 256
     arrive(2, 9)
+    for f in fetches[9:]:
+        f.start()
     for k in range(slices):
         a2[k] = decay_ref[:, k * LANES : (k + 1) * LANES] * (-LOG2E)
 
@@ -215,50 +218,65 @@
             for k in range(half):
                 hin[branch, part * half + k] = main[part][branch][:, k * LANES : (k + 1) * LANES]
 
-    to_right.wait()
-    to_left.wait()
-    border = halo[...]
-    near = border[0].astype(F32)
-    far_side = border[1]
-    far32 = far_side.astype(F32)
-    ahead = (near * inv_rms(near) * gain).astype(BF16)
-    behind = (flip_lanes(far_side, anti) * inv_rms(far32) * gain).astype(BF16)
-    has_left = (index > 0).astype(F32)
-    has_right = (index < count - 1).astype(F32)
-
-    def border_front(i, _):
-        cols = pl.ds(pl.multiple_of(i * wide, wide), wide)
-        weights = in_ref[:, cols]
-        v = dot(ahead, weights)[edge_rows - ROWS :] * has_left
-        joined = jnp.concatenate([v, edge[0, :, cols]], axis=0)
-        u_s[0, 0:ROWS, cols] = convolve(joined, 0, cols).astype(F32)[ROWS:]
-        v = dot(behind, weights)[:ROWS] * has_right
-        joined = jnp.concatenate([edge[1, :, cols], v], axis=0)
-        u_s[1, tokens - ROWS : tokens, cols] = convolve(joined, 1, cols).astype(F32)[:ROWS]
-        return 0
-
-    lax.fori_loop(0, inner_width // wide, border_front, 0)
-    border_u = jnp.concatenate([u_s[0, 0:ROWS], u_s[1, tokens - ROWS : tokens]], axis=0)
-    border_p = dot_nt(border_u.astype(BF16), sp_ref[...])
-    proj[0, 0:ROWS] = border_p[:ROWS]
-    proj[1, tokens - ROWS : tokens] = border_p[ROWS:]
-    border_dt = softplus(dot(border_p[:, :rank].astype(BF16), tp_ref[...]) + tb_ref[...])
-    border_du = border_dt * border_u
-    dt_s[0, 0:ROWS] = border_dt[:ROWS]
-    dt_s[1, tokens - ROWS : tokens] = border_dt[ROWS:]
-    none = jnp.zeros((tokens - ROWS, inner_width), F32)
-    du_s[0] = jnp.concatenate([border_du[:ROWS], none], axis=0).astype(BF16)
-    du_s[1] = jnp.concatenate([none, border_du[ROWS:]], axis=0).astype(BF16)
-    turn_proj()
-    start = scan(0, 1, ROWS)
-
-    def wide_tile(rows):
-        return jnp.concatenate(rows + [jnp.zeros((16 - len(rows), LANES), F32)], axis=0)
-
     main_tot = [
         jnp.sum(dt_s[0, ROWS:tokens], axis=0, keepdims=True),
         jnp.sum(dt_s[1, 0 : tokens - ROWS], axis=0, keepdims=True),
     ]
+    for branch in range(2):
+        for k in range(slices):
+            main_gone[branch, k] = jnp.exp2(main_tot[branch][:, k * LANES : (k + 1) * LANES] * a2[k])
+
+    to_right.wait()
+    to_left.wait()
+    border = halo[...]
+    near = border[0, edge_rows - ROWS :].astype(F32)
+    far_side = border[1]
+    far32 = far_side.astype(F32)
+    ahead = near * inv_rms(near) * gain
+    behind = (flip_lanes(far_side, anti) * inv_rms(far32) * gain)[:ROWS]
+    both = jnp.concatenate([ahead, behind], axis=0).astype(BF16)
+    has_left = (index > 0).astype(F32)
+    has_right = (index < count - 1).astype(F32)
+    border_wide = 512
+
+    def border_front(i, _):
+        cols = pl.ds(pl.multiple_of(i * border_wide, border_wide), border_wide)
+        v = dot(both, in_ref[:, cols])
+        joined = jnp.concatenate([v[:ROWS] * has_left, edge[0, :, cols]], axis=0)
+        u_s[0, 0:ROWS, cols] = convolve(joined, 0, cols).astype(F32)[ROWS:]
+        joined = jnp.concatenate([edge[1, :, cols], v[ROWS:] * has_right], axis=0)
+        u_s[1, tokens - ROWS : tokens, cols] = convolve(joined, 1, cols).astype(F32)[:ROWS]
+        return 0
+
+    lax.fori_loop(0, inner_width // border_wide, border_front, 0)
+    border_u = jnp.concatenate([u_s[0, 0:ROWS], u_s[1, tokens - ROWS : tokens]], axis=0)
+    border_b = border_u.astype(BF16)
+    border_p = dot_nt(border_b, sp_ref[...])
+    border_maps = dot_nt(sp_ref[rank : rank + states, :], border_b)
+    proj[0, 0:ROWS] = border_p[:ROWS]
+    proj[1, tokens - ROWS : tokens] = border_p[ROWS:]
+    border_dt = softplus(dot(border_p[:, :rank].astype(BF16), tp_ref[...]) + tb_ref[...])
+    border_du = (border_dt * border_u).astype(BF16)
+    dt_s[0, 0:ROWS] = border_dt[:ROWS]
+    dt_s[1, tokens - ROWS : tokens] = border_dt[ROWS:]
+    border_lane = lax.broadcasted_iota(jnp.int32, (states, 2 * ROWS), 1)
+    start = []
+    for branch in range(2):
+        spots = [j if branch == 0 else 2 * ROWS - 1 - j for j in range(ROWS)]
+        tiles = [jnp.where(border_lane == spot, border_maps, 0.0) for spot in spots]
+        new = dot(jnp.concatenate(tiles, axis=0).astype(BF16), border_du)
+        h = new[:states]
+        for j, spot in enumerate(spots):
+            t = spot if branch == 0 else tokens - 2 * ROWS + spot
+            if j:
+                dt = jnp.broadcast_to(dt_s[branch, t : t + 1, :], (states, inner_width))
+                h = jnp.exp2(dt * a2_wide()) * h + new[j * states : (j + 1) * states]
+            hist[branch, t * states : (t + 1) * states, :] = h.astype(BF16)
+        start.append(h)
+
+    def wide_tile(rows):
+        return jnp.concatenate(rows + [jnp.zeros((16 - len(rows), LANES), F32)], axis=0)
+
     start_tot = [
         jnp.sum(border_dt[:ROWS], axis=0, keepdims=True),
         jnp.sum(border_dt[ROWS:], axis=0, keepdims=True),
@@ -273,23 +291,20 @@
 
     for k in range(slices):
         lanes = slice(k * LANES, (k + 1) * LANES)
-        part, inside = divmod(k, half)
-        own = slice(inside * LANES, (inside + 1) * LANES)
-        for branch in range(2):
-            first = start[part][branch][:, own]
-            grown = jnp.exp2(main_tot[branch][:, lanes] * a2[k]) * first + hin[branch, k]
+        for branch in range(2):
+            first = start[branch][:, lanes]
+            grown = main_gone[branch, k] * first + hin[branch, k]
             send_a[k, branch] = grown.astype(BF16)
-            hist_keep = first
-            hin[branch, k] = hist_keep
+            hin[branch, k] = first
         send_a[k, 2] = tot_rows([(main_tot[b] + start_tot[b])[:, lanes] for b in range(2)])
         for branch in range(2):
             first_tot[k, branch] = jnp.broadcast_to(start_tot[branch][:, lanes], (ROWS, LANES))
 
     copies_a = []
-    for d, peer in enumerate(members):
-        target = (place + d + 1) % GROUP
+    for d in FARTHEST:
+        target = (place + d) % GROUP
         copies_a.append(
-            remote(send_a.at[target], recv_a.at[place], a_send.at[d], a_recv.at[d], peer)
+            remote(send_a.at[target], recv_a.at[place], a_send.at[d - 1], a_recv.at[d - 1], members[d - 1])
         )
     for c in copies_a:
         c.start()
@@ -379,11 +394,11 @@
 
     pl.semaphore_wait(go, len(near_z))
     copies_z = []
-    for d, peer in enumerate(distant):
+    for d in (1, 0, 2):
         target = (far + d + 1) % FAR
         branch = (target < far).astype(jnp.int32)
         copies_z.append(
-            remote(send_z.at[branch], recv_z.at[far], z_send.at[d], z_recv.at[d], peer)
+            remote(send_z.at[branch], recv_z.at[far], z_send.at[d], z_recv.at[d], distant[d])
         )
     for c in copies_z:
         c.start()
@@ -411,7 +426,7 @@
             send_c.at[target], recv_c.at[place], c_send.at[d - 1], c_recv.at[d - 1], far * GROUP + target
         )
 
-    for d in range(1, GROUP):
+    for d in FARTHEST:
         back(d).start()
     recv_c[place] = send_c[place]
 
@@ -440,13 +455,15 @@
                     ).astype(BF16)
                     pieces = []
 
-    def finish_next(d, _):
+    def finish_next(i, _):
+        odd = i % 2
+        d = (1 - odd) * (i // 2 + 1) + odd * (GROUP - (i + 1) // 2)
         back(d).wait()
         finish((place + GROUP - d) % GROUP)
         return 0
 
     finish(place)
-    lax.fori_loop(1, GROUP, finish_next, 0)
+    lax.fori_loop(0, GROUP - 1, finish_next, 0)
     forward = dot(gmix[0], out_ref[...]).astype(BF16)
     flipped = flip_lanes(dot(gmix[1], out_ref[...]).astype(BF16), anti)
     o_ref[...] = forward.astype(F32) + flipped
@@ -502,6 +519,7 @@
         pltpu.VMEM((GROUP, 2, states, LANES), BF16),
         pltpu.VMEM((2, slices, states, LANES), F32),
         pltpu.VMEM((slices, 2, ROWS, LANES), F32),
+        pltpu.VMEM((2, slices, states, LANES), F32),
         pltpu.SemaphoreType.DMA((2,)),
         pltpu.SemaphoreType.DMA((2,)),
         pltpu.SemaphoreType.DMA((GROUP - 1,)),

time: 41.3 us -> 40.4 us (0.978)
  Pallas kernels: 39.5 us -> 38.6 us
    pallas_call x1, Pallas kernels: 39.5 us -> 38.6 us  [shards(): pl.pallas_call(kernel, out_shape=jax.ShapeDtypeStruct((tokens, width), F3...]
where the time goes in v4:
time: 40.4 us; the launch traced here: 40.3 us
  Pallas kernels  38.6 us (96%)
  other arithmetic  1.63 us (4%)
    pallas_call x1, Pallas kernels, shards(): pl.pallas_call(kernel, out_shape=jax.ShapeDtypeStruct((tokens, width), F3...  38.6 us
    convert_element_type x1, other arithmetic, shards(): return (residual_stream.astype(F32) + mixed).astype(BF16)  1.63 us

profile of v4, /device:TPU:1, one launch (start us, length us, event | category | flops | bytes accessed | tf_op | source)
XLA Modules:
  0.0 40.3 jit_solution(3981087803210367142)
XLA Ops:
  0.0 0.0 copy-start
  0.0 38.6 %shard_map.109 = f32[128,512]{1,0:T(8,128)} custom-call(bf16[128,512]{1,0:T(8,128)(2,1)} %x_hbm.1, f32[1,512]{1,0:T(1,128)} %bitcast.11, bf16[512,2048]{1,0:T(8,128)(2,1)} %in_hbm.1, f32[4,1024]{1,0:T(4,128)} %cw_hbm.1, f32[1,1024]{1,0:T(1,128)} %bitcast.8, bf16[64,1024]{1,0:T(8,128)(2,1)} %bitcast.6, bf16[32,1024]{1,0:T(8,128)(2,1)} %tp_hbm.1, ...), custom_call_target="tpu_custom_call" | custom-call | tf_op jit(solution)/shard_map/pallas_call | solution.py:534
  38.6 0.0 copy-done
  38.6 1.6 %add_convert_fusion = bf16[128,512]{1,0:T(8,128)(2,1)} fusion(f32[128,512]{1,0:T(8,128)} %shard_map.109, bf16[128,512]{1,0:T(8,128)(2,1)S(1)} %copy-done), kind=kLoop, calls=%fused_computation | loop fusion | flops 196608 | bytes 524288 | tf_op jit(solution)/shard_map/convert_element_type | solution.py:556
Async XLA Ops:
  0.0 38.6 %copy-start = (bf16[128,512]{1,0:T(8,128)(2,1)S(1)}, bf16[128,512]{1,0:T(8,128)(2,1)}, u32[]{:S(2)}) copy-start(bf16[128,512]{1,0:T(8,128)(2,1)} %x_hbm.1) | copy-start | bytes 393220

commit v5 on v4

--- a/solution.py
+++ b/solution.py
@@ -17,7 +17,7 @@
 ROWS = 8
 FARTHEST = (4, 3, 5, 2, 6, 1, 7)
 SCAN = 40
-EARLY = 7
+EARLY = 4
 
 
 def dot(a, b):
@@ -60,7 +60,7 @@
     x_hbm, gain_hbm, in_hbm, cw_hbm, cb_hbm, sp_hbm, tp_hbm, tb_hbm, decay_hbm, skip_hbm, out_hbm,
     o_ref,
     x_ref, gain_ref, in_ref, gate_ref, cw_ref, cb_ref, sp_ref, tp_ref, tb_ref, decay_ref, skip_ref, out_ref,
-    halo, nrm, a2, edge, u_s, proj, proj_t, dt_s, du_s, hist, cblk, cum, gc, pre, sg, gmix,
+    halo, nrm, a2, edge, u_s, proj, proj_t, dt_s, du_s, hist, cblk, cum, gc, pre, sg, added_up,
     send_a, recv_a, send_z, recv_z, send_c, recv_c, hin, first_tot, main_gone,
     halo_send, halo_recv, a_send, a_recv, z_send, z_recv, c_send, c_recv, fetched, go,
 ):
@@ -432,7 +432,9 @@
 
     def finish(k):
         cols = pl.ds(pl.multiple_of(k * LANES, LANES), LANES)
-        for branch in range(2):
+        both = []
+        for branch in range(2):
+            mixes = []
             edge_h = recv_c[k, branch].astype(F32)
             gone = jnp.exp2(first_tot[k, branch, 0:1, :] * a2[k])
             main_h = gone * edge_h + hin[branch, k]
@@ -450,22 +452,31 @@
                     total = total + gc[branch, k, n, rows, :] * h
                 pieces.append(total * sg[branch, rows, cols])
                 if len(pieces) == 2:
-                    gmix[branch, (b - 1) * ROWS : (b + 1) * ROWS, cols] = jnp.concatenate(
-                        pieces, axis=0
-                    ).astype(BF16)
+                    mixes.append(jnp.concatenate(pieces, axis=0).astype(BF16))
                     pieces = []
-
-    def finish_next(i, _):
-        odd = i % 2
-        d = (1 - odd) * (i // 2 + 1) + odd * (GROUP - (i + 1) // 2)
+            both.append(jnp.concatenate(mixes, axis=0))
+        return both, out_ref[cols, :]
+
+    def add_up(one, other, first=False):
+        weights = jnp.concatenate([one[1], other[1]], axis=0)
+        for branch in range(2):
+            share = dot(jnp.concatenate([one[0][branch], other[0][branch]], axis=1), weights)
+            added_up[branch] = share if first else added_up[branch] + share
+
+    def arrived(d):
         back(d).wait()
-        finish((place + GROUP - d) % GROUP)
-        return 0
-
-    finish(place)
-    lax.fori_loop(0, GROUP - 1, finish_next, 0)
-    forward = dot(gmix[0], out_ref[...]).astype(BF16)
-    flipped = flip_lanes(dot(gmix[1], out_ref[...]).astype(BF16), anti)
+        return finish((place + GROUP - d) % GROUP)
+
+    def finish_pair(i, _):
+        one = arrived(GROUP - 1 - i)
+        add_up(one, arrived(2 + i))
+        return 0
+
+    own = finish(place)
+    add_up(own, arrived(1), True)
+    lax.fori_loop(0, GROUP // 2 - 1, finish_pair, 0)
+    forward = added_up[0].astype(BF16)
+    flipped = flip_lanes(added_up[1].astype(BF16), anti)
     o_ref[...] = forward.astype(F32) + flipped
 
 
@@ -510,7 +521,7 @@
         pltpu.VMEM((2, slices, states, tokens, LANES), F32),
         pltpu.VMEM(by_token, F32),
         pltpu.VMEM(by_token, F32),
-        pltpu.VMEM(by_token, BF16),
+        pltpu.VMEM((2, tokens, width), F32),
         pltpu.VMEM((GROUP, 3, states, LANES), BF16),
         pltpu.VMEM((GROUP, 3, states, LANES), BF16),
         pltpu.VMEM((2, 2, states, LANES), BF16),

time: 40.4 us -> 39.7 us (0.983)
  Pallas kernels: 38.6 us -> 37.9 us
    pallas_call x1, Pallas kernels: 38.6 us -> 37.9 us  [shards(): pl.pallas_call(kernel, out_shape=jax.ShapeDtypeStruct((tokens, width), F3...]
where the time goes in v5:
time: 39.7 us; the launch traced here: 39.6 us
  Pallas kernels  37.9 us (95%)
  other arithmetic  1.63 us (4%)
    pallas_call x1, Pallas kernels, shards(): pl.pallas_call(kernel, out_shape=jax.ShapeDtypeStruct((tokens, width), F3...  37.9 us
    convert_element_type x1, other arithmetic, shards(): return (residual_stream.astype(F32) + mixed).astype(BF16)  1.63 us

profile of v5, /device:TPU:1, one launch (start us, length us, event | category | flops | bytes accessed | tf_op | source)
XLA Modules:
  0.0 39.6 jit_solution(6973454611752091678)
XLA Ops:
  0.0 0.0 copy-start
  0.0 37.9 %shard_map.109 = f32[128,512]{1,0:T(8,128)} custom-call(bf16[128,512]{1,0:T(8,128)(2,1)} %x_hbm.1, f32[1,512]{1,0:T(1,128)} %bitcast.11, bf16[512,2048]{1,0:T(8,128)(2,1)} %in_hbm.1, f32[4,1024]{1,0:T(4,128)} %cw_hbm.1, f32[1,1024]{1,0:T(1,128)} %bitcast.8, bf16[64,1024]{1,0:T(8,128)(2,1)} %bitcast.6, bf16[32,1024]{1,0:T(8,128)(2,1)} %tp_hbm.1, ...), custom_call_target="tpu_custom_call" | custom-call | tf_op jit(solution)/shard_map/pallas_call | solution.py:545
  37.9 0.0 copy-done
  37.9 1.6 %add_convert_fusion = bf16[128,512]{1,0:T(8,128)(2,1)} fusion(f32[128,512]{1,0:T(8,128)} %shard_map.109, bf16[128,512]{1,0:T(8,128)(2,1)S(1)} %copy-done), kind=kLoop, calls=%fused_computation | loop fusion | flops 196608 | bytes 524288 | tf_op jit(solution)/shard_map/convert_element_type | solution.py:567
Async XLA Ops:
  0.0 37.9 %copy-start = (bf16[128,512]{1,0:T(8,128)(2,1)S(1)}, bf16[128,512]{1,0:T(8,128)(2,1)}, u32[]{:S(2)}) copy-start(bf16[128,512]{1,0:T(8,128)(2,1)} %x_hbm.1) | copy-start | bytes 393220
